TPU v7x, 256 devices: a whole 4x4x8 slice. The times are simulated.
256 devices in a mesh: grp: 8 (over x, core), lx: 4 (over y), ly: 8 (over z).
Axes of the slice: x: 4, y: 4, z: 8, core: 2. Of those that a mesh axis runs over, the one named last changes fastest.
Arguments:
- vectors: float32 [32, 256, 4096], P('grp', 'lx', 'ly'), may hold values from -6 to 6
- levels: int32 [256, 4096], P('lx', 'ly'), may hold values from 0 to 7
- level_table: float32 [8], replicated, may hold values from 1 to 3
- filter_low: float32 [1], replicated, may hold values from -1 to 0.5
- filter_high: float32 [1], replicated, may hold values from 6 to 7.5
Outputs:
- basis: float32 [32, 256, 4096], P('grp', 'lx', 'ly')
All inputs are finite; a program needn't handle non-finite values.
Results may differ from a plain program's by a relative error of at most 0.00011.
Values sent between devices are 32-bit elements; how exact they have to be, the bound alone decides.
No kernel may reach another device: no remote copies, remote signals or barrier semaphores. Data moves between devices by JAX's collectives and lax.ppermute only.
A program may use at most 64 MiB of HBM per device.

v0:
```python
import jax
import jax.numpy as jnp
from jax import lax
from jax.sharding import PartitionSpec as P


def padded_2(shard, sides, width):
    for axis, dim in sides:
        size, length = (lax.axis_size(axis), shard.shape[dim])
        up = [(i, (i + 1) % size) for i in range(size)]
        down = [(j, i) for i, j in up]
        last = lax.slice_in_dim(shard, length - width, length, axis=dim)
        leading = lax.slice_in_dim(shard, 0, width, axis=dim)
        before = lax.ppermute(last, axis, up)
        after = lax.ppermute(leading, axis, down)
        shard = jnp.concatenate([before, shard, after], axis=dim)
    return shard


def from_root(value, axis, source):
    kept = jnp.where(lax.axis_index(axis) == source, value, 0).astype(value.dtype)
    return lax.psum(kept, axis)


def apply_operator(field, onsite):
    padded = padded_2(field, (("lx", 1), ("ly", 2)), 1)
    beside = padded[:, 2:, 1:-1] + padded[:, :-2, 1:-1] + padded[:, 1:-1, 2:] + padded[:, 1:-1, :-2]
    return onsite[None] * field - beside


def lower_inverse(gram):
    lower = jnp.linalg.cholesky(gram)
    eye_block = jnp.eye(gram.shape[0], dtype=jnp.float32)
    return lax.linalg.triangular_solve(lower, eye_block, left_side=True, lower=True)


def body(vectors, levels, level_table, filter_low, filter_high):
    count_vec, rows_local, cols_local = vectors.shape
    level_ids = jnp.arange(level_table.shape[0], dtype=jnp.int32)
    onsite = jnp.sum(
        jnp.where(levels[None] == level_ids[:, None, None], level_table[:, None, None], 0.0), axis=0
    )
    center = (filter_high[0] + filter_low[0]) / 2.0
    half = (filter_high[0] - filter_low[0]) / 2.0
    first = (apply_operator(vectors, onsite) - center * vectors) / half
    filtered = 2.0 * (apply_operator(first, onsite) - center * first) / half - vectors
    total = rows_local * cols_local * lax.axis_size("lx") * lax.axis_size("ly")
    flat = filtered.reshape(count_vec, rows_local * cols_local)
    highest = lax.Precision.HIGHEST
    mine = lax.axis_index("grp")
    result = jnp.zeros_like(flat)
    for h in range(lax.axis_size("grp")):
        gram = lax.psum(jnp.dot(flat, flat.T, precision=highest), ("lx", "ly")) / total
        done = jnp.dot(lower_inverse(gram), flat, precision=highest)
        result = jnp.where(mine == h, done, result)
        shared = from_root(done, "grp", h)
        coeff = lax.psum(jnp.dot(shared, flat.T, precision=highest), ("lx", "ly")) / total
        later = mine > h
        flat = jnp.where(later, flat - jnp.dot(coeff.T, shared, precision=highest), flat)
    return result.reshape(count_vec, rows_local, cols_local)


def solution(mesh):
    in_specs = (P("grp", "lx", "ly"), P("lx", "ly"), P(), P(), P())
    out_specs = P("grp", "lx", "ly")
    return jax.shard_map(body, mesh=mesh, in_specs=in_specs, out_specs=out_specs, check_vma=False)
```

profile of v0, /device:TPU:32, one launch (start us, length us, event | category | flops | bytes accessed | tf_op | source)
XLA Modules:
  0.0 1632.8 jit_solution(7607256732290742390)
XLA Ops:
  7.4 3.1 collective-permute-start
  10.5 1.4 collective-permute-done
  11.9 3.5 collective-permute-done.1
  15.4 1.1 pad_maximum_fusion.21
  16.7 1.9 collective-permute-start.3
  20.1 1.6 collective-permute-done.2
  21.7 3.9 collective-permute-done.3
  26.2 2.0 collective-permute-start.5
  28.2 1.6 collective-permute-done.4
  29.8 1.3 collective-permute-done.5
  31.3 3.3 collective-permute-start.6
  34.6 2.7 collective-permute-done.6
  37.3 2.5 collective-permute-done.7
  40.2 2.4 convolution_bitcast_fusion
  42.6 71.0 %psum.154 = f32[4,4]{0,1:T(4,128)S(1)} all-reduce(f32[4,4]{0,1:T(4,128)S(1)} %convolution_bitcast_fusion), channel_id=1, replica_groups=mesh['grp'=8,'lx'=4,'ly'=8] {'lx','ly'}, use_global_device_ids=true, to_apply=%region_1.2 | all-reduce | flops 16 | bytes 128 | tf_op jit(solution)/shard_map/psum | solution.py:53
  116.2 1.8 convolution_select_fusion.1
  118.3 60.3 %all-reduce.8.cloned.1.call-done = f32[4,32768]{1,0:T(4,128)} async-done(((f32[4,32768]{1,0:T(4,128)}), f32[4,32768]{1,0:T(4,128)}) %all-reduce.8.cloned.1.call-update) | async-done | bytes 524304 | tf_op jit(solution)/shard_map/psum | solution.py:22
  178.6 3.5 fusion.99
  182.1 71.6 %psum.156 = f32[4,4]{0,1:T(4,128)S(1)} all-reduce(f32[4,4]{0,1:T(4,128)S(1)} %fusion.99), channel_id=1, replica_groups=mesh['grp'=8,'lx'=4,'ly'=8] {'lx','ly'}, use_global_device_ids=true, to_apply=%region_5.8 | all-reduce | flops 16 | bytes 128 | tf_op jit(solution)/shard_map/psum | solution.py:57
  253.7 1.0 fusion.6
  254.8 2.3 fusion.100
  257.1 73.6 %psum.157 = f32[4,4]{0,1:T(4,128)S(1)} all-reduce(f32[4,4]{0,1:T(4,128)S(1)} %fusion.100), channel_id=1, replica_groups=mesh['grp'=8,'lx'=4,'ly'=8] {'lx','ly'}, use_global_device_ids=true, to_apply=%region_6.9 | all-reduce | flops 16 | bytes 128 | tf_op jit(solution)/shard_map/psum | solution.py:53
  333.1 1.8 broadcast_select_fusion.5
  335.0 58.1 %all-reduce.10.cloned.1.call-done = f32[4,32768]{1,0:T(4,128)} async-done(((f32[4,32768]{1,0:T(4,128)}), f32[4,32768]{1,0:T(4,128)}) %all-reduce.10.cloned.1.call-update) | async-done | bytes 524304 | tf_op jit(solution)/shard_map/psum | solution.py:22
  393.1 3.5 fusion.101
  396.6 71.6 %psum.159 = f32[4,4]{0,1:T(4,128)S(1)} all-reduce(f32[4,4]{0,1:T(4,128)S(1)} %fusion.101), channel_id=1, replica_groups=mesh['grp'=8,'lx'=4,'ly'=8] {'lx','ly'}, use_global_device_ids=true, to_apply=%region_8.11 | all-reduce | flops 16 | bytes 128 | tf_op jit(solution)/shard_map/psum | solution.py:57
  468.2 1.0 fusion.5
  469.2 2.3 fusion.102
  471.6 73.6 %psum.160 = f32[4,4]{0,1:T(4,128)S(1)} all-reduce(f32[4,4]{0,1:T(4,128)S(1)} %fusion.102), channel_id=1, replica_groups=mesh['grp'=8,'lx'=4,'ly'=8] {'lx','ly'}, use_global_device_ids=true, to_apply=%region_9.12 | all-reduce | flops 16 | bytes 128 | tf_op jit(solution)/shard_map/psum | solution.py:53
  547.6 1.8 broadcast_select_fusion.4
  549.8 57.8 %all-reduce.12.cloned.1.call-done = f32[4,32768]{1,0:T(4,128)} async-done(((f32[4,32768]{1,0:T(4,128)}), f32[4,32768]{1,0:T(4,128)}) %all-reduce.12.cloned.1.call-update) | async-done | bytes 524304 | tf_op jit(solution)/shard_map/psum | solution.py:22
  607.6 3.5 fusion.103
  611.1 71.6 %psum.162 = f32[4,4]{0,1:T(4,128)S(1)} all-reduce(f32[4,4]{0,1:T(4,128)S(1)} %fusion.103), channel_id=1, replica_groups=mesh['grp'=8,'lx'=4,'ly'=8] {'lx','ly'}, use_global_device_ids=true, to_apply=%region_11.14 | all-reduce | flops 16 | bytes 128 | tf_op jit(solution)/shard_map/psum | solution.py:57
  682.7 1.0 fusion.4
  683.7 2.3 fusion.104
  686.1 73.6 %psum.163 = f32[4,4]{0,1:T(4,128)S(1)} all-reduce(f32[4,4]{0,1:T(4,128)S(1)} %fusion.104), channel_id=1, replica_groups=mesh['grp'=8,'lx'=4,'ly'=8] {'lx','ly'}, use_global_device_ids=true, to_apply=%region_12.15 | all-reduce | flops 16 | bytes 128 | tf_op jit(solution)/shard_map/psum | solution.py:53
  762.1 1.8 broadcast_select_fusion.3
  764.0 58.1 %all-reduce.14.cloned.1.call-done = f32[4,32768]{1,0:T(4,128)} async-done(((f32[4,32768]{1,0:T(4,128)}), f32[4,32768]{1,0:T(4,128)}) %all-reduce.14.cloned.1.call-update) | async-done | bytes 524304 | tf_op jit(solution)/shard_map/psum | solution.py:22
  822.1 3.5 fusion.105
  825.6 71.6 %psum.165 = f32[4,4]{0,1:T(4,128)S(1)} all-reduce(f32[4,4]{0,1:T(4,128)S(1)} %fusion.105), channel_id=1, replica_groups=mesh['grp'=8,'lx'=4,'ly'=8] {'lx','ly'}, use_global_device_ids=true, to_apply=%region_14.17 | all-reduce | flops 16 | bytes 128 | tf_op jit(solution)/shard_map/psum | solution.py:57
  898.2 2.3 fusion.106
  900.6 73.6 %psum.166 = f32[4,4]{0,1:T(4,128)S(1)} all-reduce(f32[4,4]{0,1:T(4,128)S(1)} %fusion.106), channel_id=1, replica_groups=mesh['grp'=8,'lx'=4,'ly'=8] {'lx','ly'}, use_global_device_ids=true, to_apply=%region_15.18 | all-reduce | flops 16 | bytes 128 | tf_op jit(solution)/shard_map/psum | solution.py:53
  976.6 1.8 broadcast_select_fusion.2
  978.9 57.6 %all-reduce.16.cloned.1.call-done = f32[4,32768]{1,0:T(4,128)} async-done(((f32[4,32768]{1,0:T(4,128)}), f32[4,32768]{1,0:T(4,128)}) %all-reduce.16.cloned.1.call-update) | async-done | bytes 524304 | tf_op jit(solution)/shard_map/psum | solution.py:22
  1036.6 3.5 fusion.107
  1040.0 71.6 %psum.168 = f32[4,4]{0,1:T(4,128)S(1)} all-reduce(f32[4,4]{0,1:T(4,128)S(1)} %fusion.107), channel_id=1, replica_groups=mesh['grp'=8,'lx'=4,'ly'=8] {'lx','ly'}, use_global_device_ids=true, to_apply=%region_17.20 | all-reduce | flops 16 | bytes 128 | tf_op jit(solution)/shard_map/psum | solution.py:57
  1111.6 2.0 fusion.2
  1113.7 2.3 fusion.108
  1116.0 73.6 %psum.169 = f32[4,4]{0,1:T(4,128)S(1)} all-reduce(f32[4,4]{0,1:T(4,128)S(1)} %fusion.108), channel_id=1, replica_groups=mesh['grp'=8,'lx'=4,'ly'=8] {'lx','ly'}, use_global_device_ids=true, to_apply=%region_18.21 | all-reduce | flops 16 | bytes 128 | tf_op jit(solution)/shard_map/psum | solution.py:53
  1192.1 2.0 broadcast_select_fusion.1
  1194.2 58.1 %all-reduce.18.cloned.1.call-done = f32[4,32768]{1,0:T(4,128)} async-done(((f32[4,32768]{1,0:T(4,128)}), f32[4,32768]{1,0:T(4,128)}) %all-reduce.18.cloned.1.call-update) | async-done | bytes 524304 | tf_op jit(solution)/shard_map/psum | solution.py:22
  1252.2 3.5 fusion.109
  1255.7 71.6 %psum.171 = f32[4,4]{0,1:T(4,128)S(1)} all-reduce(f32[4,4]{0,1:T(4,128)S(1)} %fusion.109), channel_id=1, replica_groups=mesh['grp'=8,'lx'=4,'ly'=8] {'lx','ly'}, use_global_device_ids=true, to_apply=%region_20.23 | all-reduce | flops 16 | bytes 128 | tf_op jit(solution)/shard_map/psum | solution.py:57
  1327.3 2.0 fusion.1
  1329.3 2.3 fusion.110
  1331.6 73.8 %psum.172 = f32[4,4]{0,1:T(4,128)S(1)} all-reduce(f32[4,4]{0,1:T(4,128)S(1)} %fusion.110), channel_id=1, replica_groups=mesh['grp'=8,'lx'=4,'ly'=8] {'lx','ly'}, use_global_device_ids=true, to_apply=%region_21.24 | all-reduce | flops 16 | bytes 128 | tf_op jit(solution)/shard_map/psum | solution.py:53
  1407.9 2.0 broadcast_select_fusion
  1409.9 58.1 %all-reduce.20.cloned.1.call-done = f32[4,32768]{1,0:T(4,128)} async-done(((f32[4,32768]{1,0:T(4,128)}), f32[4,32768]{1,0:T(4,128)}) %all-reduce.20.cloned.1.call-update) | async-done | bytes 524304 | tf_op jit(solution)/shard_map/psum | solution.py:22
  1468.0 3.5 fusion.111
  1471.5 71.6 %psum.174 = f32[4,4]{0,1:T(4,128)S(1)} all-reduce(f32[4,4]{0,1:T(4,128)S(1)} %fusion.111), channel_id=1, replica_groups=mesh['grp'=8,'lx'=4,'ly'=8] {'lx','ly'}, use_global_device_ids=true, to_apply=%region_23.26 | all-reduce | flops 16 | bytes 128 | tf_op jit(solution)/shard_map/psum | solution.py:57
  1543.1 2.0 fusion
  1545.1 2.3 fusion.112
  1547.5 73.6 %psum.175 = f32[4,4]{0,1:T(4,128)S(1)} all-reduce(f32[4,4]{0,1:T(4,128)S(1)} %fusion.112), channel_id=1, replica_groups=mesh['grp'=8,'lx'=4,'ly'=8] {'lx','ly'}, use_global_device_ids=true, to_apply=%region_24.27 | all-reduce | flops 16 | bytes 128 | tf_op jit(solution)/shard_map/psum | solution.py:53
  1623.5 1.3 convolution_select_fusion
  (115 shorter events, 25.3 us)
Async XLA Ops:
  6.5 172.1 %all-reduce.8.cloned.1.call-start = ((), (), s32[]{:S(2)}) async-start(), calls=%async_computation | async-start | bytes 1048576 | tf_op jit(solution)/shard_map/psum | solution.py:22
  7.4 4.5 collective-permute-start
  10.5 8.1 copy-start.6
  10.5 15.1 copy-start
  10.5 4.9 collective-permute-start.1
  16.5 2.1 copy-start.7
  16.5 5.2 collective-permute-start.2
  16.7 9.0 collective-permute-start.3
  26.1 3.7 collective-permute-start.4
  26.2 4.9 collective-permute-start.5
  31.3 6.0 collective-permute-start.6
  34.6 5.1 collective-permute-start.7
  118.0 275.1 %all-reduce.10.cloned.1.call-start = ((), (), s32[]{:S(2)}) async-start(), calls=%async_computation.1 | async-start | bytes 1048576 | tf_op jit(solution)/shard_map/psum | solution.py:22
  178.6 75.1 %copy-start.5 = (f32[4,32768]{1,0:T(4,128)S(1)}, f32[4,32768]{1,0:T(4,128)}, u32[]{:S(2)}) copy-start(f32[4,32768]{1,0:T(4,128)} %all-reduce.8.cloned.1.call-done) | copy-start | bytes 1572868
  335.0 272.6 %all-reduce.12.cloned.1.call-start = ((), (), s32[]{:S(2)}) async-start(), calls=%async_computation.2 | async-start | bytes 1048576 | tf_op jit(solution)/shard_map/psum | solution.py:22
  393.1 75.1 %copy-start.2 = (f32[4,32768]{1,0:T(4,128)S(1)}, f32[4,32768]{1,0:T(4,128)}, u32[]{:S(2)}) copy-start(f32[4,32768]{1,0:T(4,128)} %all-reduce.10.cloned.1.call-done) | copy-start | bytes 1572868
  549.5 272.6 %all-reduce.14.cloned.1.call-start = ((), (), s32[]{:S(2)}) async-start(), calls=%async_computation.3 | async-start | bytes 1048576 | tf_op jit(solution)/shard_map/psum | solution.py:22
  607.6 75.1 %copy-start.3 = (f32[4,32768]{1,0:T(4,128)S(1)}, f32[4,32768]{1,0:T(4,128)}, u32[]{:S(2)}) copy-start(f32[4,32768]{1,0:T(4,128)} %all-reduce.12.cloned.1.call-done) | copy-start | bytes 1572868
  764.0 272.6 %all-reduce.16.cloned.1.call-start = ((), (), s32[]{:S(2)}) async-start(), calls=%async_computation.4 | async-start | bytes 1048576 | tf_op jit(solution)/shard_map/psum | solution.py:22
  822.1 75.1 %copy-start.4 = (f32[4,32768]{1,0:T(4,128)S(1)}, f32[4,32768]{1,0:T(4,128)}, u32[]{:S(2)}) copy-start(f32[4,32768]{1,0:T(4,128)} %all-reduce.14.cloned.1.call-done) | copy-start | bytes 1572868
  978.5 273.7 %all-reduce.18.cloned.1.call-start = ((), (), s32[]{:S(2)}) async-start(), calls=%async_computation.5 | async-start | bytes 1048576 | tf_op jit(solution)/shard_map/psum | solution.py:22
  1194.1 273.9 %all-reduce.20.cloned.1.call-start = ((), (), s32[]{:S(2)}) async-start(), calls=%async_computation.6 | async-start | bytes 1048576 | tf_op jit(solution)/shard_map/psum | solution.py:22
  1545.1 78.4 %copy-start.1 = (f32[4,32768]{1,0:T(4,128)S(1)}, f32[4,32768]{1,0:T(4,128)}, u32[]{:S(2)}) copy-start(f32[4,32768]{1,0:T(4,128)} %convolution_select_fusion.1) | copy-start | bytes 1572868
Sparse Core Ops, SparseCore 0:
  118.2 60.3 all-reduce.7
  335.1 57.9 all-reduce.9
  549.6 57.9 all-reduce.11
  764.1 57.9 all-reduce.13
  978.6 57.9 all-reduce.15
  1194.2 57.9 all-reduce.17
  1410.0 57.9 all-reduce.19
where the time goes:
time: 1640 us; the launch traced here: 1630 us
  blocking collectives  1090 us (66%)
  waiting for transfers between devices  427 us (26%)
  matrix products  69.2 us (4%)
  other arithmetic  19.4 us (1%)
    psum x8, blocking collectives, body(): lax.psum(jnp.dot(flat, flat.T, precision=highest), ('lx', 'ly')) / total  586 us
    psum x7, blocking collectives, body(): lax.psum(jnp.dot(shared, flat.T, precision=highest), ('lx', 'ly')) / total  501 us
    psum x7, waiting for transfers between devices, from_root(): return lax.psum(kept, axis)  408 us
  transfers between devices with their start and end apart: 15, of which 15 were waited for; matrix products, arithmetic and copies ran while one was open for 0% of the time, Pallas kernels for 0%

commit v1 on v0

v1 whole, which is shorter than its diff:
```python
import jax
import jax.numpy as jnp
from jax import lax
from jax.experimental import pallas as pl
from jax.experimental.pallas import tpu as pltpu
from jax.sharding import PartitionSpec as P

HIGHEST = lax.Precision.HIGHEST
VMEM = pl.BlockSpec(memory_space=pltpu.VMEM)
SMEM = pl.BlockSpec(memory_space=pltpu.SMEM)


def shape_of(*dims):
    return jax.ShapeDtypeStruct(dims, jnp.float32)


def edge_rows_kernel(v_ref, levels_ref, table_ref, onsite_ref, first_ref, last_ref):
    levels = levels_ref[...]
    onsite = jnp.zeros(levels.shape, jnp.float32)
    for k in range(table_ref.shape[0]):
        onsite = jnp.where(levels == k, table_ref[k], onsite)
    onsite_ref[...] = onsite
    count, rows = v_ref.shape[0], v_ref.shape[1]
    for j in range(count):
        first_ref[2 * j : 2 * j + 2, :] = v_ref[j, 0:2, :]
        last_ref[2 * j : 2 * j + 2, :] = v_ref[j, rows - 2 : rows, :]
    first_ref[2 * count : 2 * count + 2, :] = onsite[0:2]
    last_ref[2 * count : 2 * count + 2, :] = onsite[rows - 2 : rows]


def halo_rows(above_ref, below_ref, j, lanes):
    width = lanes.stop - lanes.start
    gap = jnp.zeros((4, width), jnp.float32)
    return jnp.concatenate(
        [below_ref[2 * j : 2 * j + 2, lanes], gap, above_ref[2 * j : 2 * j + 2, lanes]], axis=0
    )


def edge_columns_kernel(v_ref, onsite_ref, above_ref, below_ref, first_ref, last_ref):
    count, rows, cols = v_ref.shape
    lane = lax.broadcasted_iota(jnp.int32, (rows + 8, 128), 1)
    first = jnp.zeros((rows + 8, 128), jnp.float32)
    last = jnp.zeros((rows + 8, 128), jnp.float32)
    for j in range(count + 1):
        head, tail = slice(0, 128), slice(cols - 128, cols)
        own_head = v_ref[j, :, head] if j < count else onsite_ref[:, head]
        own_tail = v_ref[j, :, tail] if j < count else onsite_ref[:, tail]
        left = jnp.concatenate([own_head, halo_rows(above_ref, below_ref, j, head)], axis=0)
        right = jnp.concatenate([own_tail, halo_rows(above_ref, below_ref, j, tail)], axis=0)
        if j:
            left = pltpu.roll(left, 2 * j, 1)
            right = pltpu.roll(right, 128 - 2 * j, 1)
        first = jnp.where(lane // 2 == j, left, first)
        last = jnp.where((127 - lane) // 2 == j, right, last)
    first_ref[...] = first
    last_ref[...] = last


def filter_kernel(v_ref, onsite_ref, above_ref, below_ref, before_ref, after_ref, low_ref, high_ref, out_ref):
    count, rows, cols = v_ref.shape
    strips = out_ref.shape[0]
    deep = rows // strips
    lane = lax.broadcasted_iota(jnp.int32, (rows + 8, 128), 1)
    wide = slice(0, cols)

    def extended(j):
        own = v_ref[j] if j < count else onsite_ref[...]
        tall = jnp.concatenate([own, halo_rows(above_ref, below_ref, j, wide)], axis=0)
        after, before = after_ref[...], before_ref[...]
        if j:
            after = pltpu.roll(after, 128 - 2 * j, 1)
            before = pltpu.roll(before, 2 * j, 1)
        side = jnp.where(lane < 64, after, before)
        return jnp.concatenate([tall, side], axis=1)

    center = (high_ref[0] + low_ref[0]) / 2.0
    half = jnp.full((1, 1), (high_ref[0] - low_ref[0]) * 0.5, jnp.float32)
    scale = 1.0 / half
    weight = (extended(count) - center) * scale

    def scaled_operator(x):
        height, width = x.shape
        beside = (pltpu.roll(x, 1, 0) + pltpu.roll(x, height - 1, 0)) + (
            pltpu.roll(x, 1, 1) + pltpu.roll(x, width - 1, 1)
        )
        return weight * x - scale * beside

    for j in range(count):
        x = extended(j)
        filtered = 2.0 * scaled_operator(scaled_operator(x)) - x
        for s in range(strips):
            out_ref[s, j] = filtered[s * deep : (s + 1) * deep, :cols]


def gram_kernel(scale, x_ref, out_ref):
    count, deep, cols = x_ref.shape
    gram = jnp.zeros((count, 128), jnp.float32)
    none = jnp.zeros((128 - count, cols), jnp.float32)
    for r in range(deep):
        x = x_ref[:, r, :]
        gram = gram + lax.dot_general(
            x, jnp.concatenate([x, none], axis=0), (((1,), (1,)), ((), ())),
            precision=HIGHEST, preferred_element_type=jnp.float32,
        )
    packed = gram[0:8]
    for q in range(1, count // 8):
        packed = packed + pltpu.roll(gram[8 * q : 8 * q + 8], q * count, 1)
    out_ref[...] = packed * scale


def combine_kernel(gram_ref, x_ref, out_ref):
    count, deep, cols = x_ref.shape
    packed = gram_ref[0]
    for k in range(1, gram_ref.shape[0]):
        packed = packed + gram_ref[k]
    pieces = [packed] + [pltpu.roll(packed, 128 - q * count, 1) for q in range(1, count // 8)]
    row = lax.broadcasted_iota(jnp.int32, (count, 128), 0)
    lane = lax.broadcasted_iota(jnp.int32, (count, 128), 1)
    work = jnp.where(lane < count, jnp.concatenate(pieces, axis=0), 0.0)
    work = jnp.where(lane == row + count, 1.0, work)
    for j in range(count):
        pivot = work[j : j + 1, :]
        factor = work[:, j : j + 1] * (1.0 / work[j : j + 1, j : j + 1])
        work = work - jnp.where(row > j, factor, 0.0) * pivot
    diagonal = jnp.sum(jnp.where(lane == row, work, 0.0), axis=1, keepdims=True)
    work = work * (1.0 / jnp.sqrt(diagonal))
    inverse = pltpu.roll(work, 128 - count, 1)[:, :count]
    for r in range(deep):
        out_ref[:, r, :] = jnp.dot(
            inverse, x_ref[:, r, :], precision=HIGHEST, preferred_element_type=jnp.float32
        )


def shifted(value, axis, step):
    size = lax.axis_size(axis)
    return lax.ppermute(value, axis, [(i, (i + step) % size) for i in range(size)])


def gathered(value, axes):
    size = lax.axis_size(axes)
    return lax.all_to_all(jnp.broadcast_to(value[None], (size,) + value.shape), axes, 0, 0)


def body(vectors, levels, level_table, filter_low, filter_high):
    count, rows, cols = vectors.shape
    groups = lax.axis_size("grp")
    every = count * groups
    deep = rows // groups
    packed_rows = 8 * ((2 * (count + 1) + 7) // 8)
    onsite, first_rows, last_rows = pl.pallas_call(
        edge_rows_kernel,
        out_shape=(shape_of(rows, cols), shape_of(packed_rows, cols), shape_of(packed_rows, cols)),
        in_specs=[VMEM, VMEM, SMEM],
        out_specs=(VMEM, VMEM, VMEM),
        name="edge_rows",
    )(vectors, levels, level_table)
    above = shifted(last_rows, "lx", 1)
    below = shifted(first_rows, "lx", -1)
    first_cols, last_cols = pl.pallas_call(
        edge_columns_kernel,
        out_shape=(shape_of(rows + 8, 128), shape_of(rows + 8, 128)),
        in_specs=[VMEM] * 4,
        out_specs=(VMEM, VMEM),
        name="edge_columns",
    )(vectors, onsite, above, below)
    before = shifted(last_cols, "ly", 1)
    after = shifted(first_cols, "ly", -1)
    strips = pl.pallas_call(
        filter_kernel,
        out_shape=shape_of(groups, count, deep, cols),
        in_specs=[VMEM] * 6 + [SMEM] * 2,
        out_specs=VMEM,
        name="filter",
    )(vectors, onsite, above, below, before, after, filter_low, filter_high)
    mine = lax.all_to_all(strips, "grp", 0, 0).reshape(every, deep, cols)
    total = rows * cols * lax.axis_size("lx") * lax.axis_size("ly")
    gram = pl.pallas_call(
        lambda *refs: gram_kernel(1.0 / total, *refs),
        out_shape=shape_of(8, 128),
        in_specs=[VMEM],
        out_specs=VMEM,
        name="gram",
    )(mine)
    gram = jnp.sum(gathered(gram, ("lx", "ly")), axis=0)
    grams = gathered(gram, "grp")
    done = pl.pallas_call(
        combine_kernel,
        out_shape=shape_of(every, deep, cols),
        in_specs=[VMEM] * 2,
        out_specs=VMEM,
        name="combine",
    )(grams, mine)
    back = lax.all_to_all(done.reshape(groups, count, deep, cols), "grp", 0, 0)
    return back.transpose(1, 0, 2, 3).reshape(count, rows, cols)


def solution(mesh):
    in_specs = (P("grp", "lx", "ly"), P("lx", "ly"), P(), P(), P())
    out_specs = P("grp", "lx", "ly")
    return jax.shard_map(body, mesh=mesh, in_specs=in_specs, out_specs=out_specs, check_vma=False)
```

time: 1640 us -> 88 us (0.05)
  the two profiles are of different devices: /device:TPU:32 before, /device:TPU:1 now
where the time goes in v1:
time: 88 us; the launch traced here: 87.6 us
  blocking collectives  57.7 us (66%)
  Pallas kernels  14.2 us (16%)
  starting transfers between devices  9.15 us (10%)
  local copies, waits for them, and re-layouts  3.37 us (4%)
  waiting for transfers between devices  1.79 us (2%)
  between operations  1.32 us (2%)
    all_to_all x2, blocking collectives, gathered(): lax.all_to_all(jnp.broadcast_to(value[None], (size,) + value.shape), axes...  27.5 us
    all_to_all x1, blocking collectives, body(): mine = lax.all_to_all(strips, 'grp', 0, 0).reshape(every, deep, cols)  16.7 us
    all_to_all x1, blocking collectives, body(): back = lax.all_to_all(done.reshape(groups, count, deep, cols), 'grp', 0, 0)  13.5 us
    ppermute x4, starting transfers between devices, shifted(): lax.ppermute(value, axis, [(i, (i + step) % size) for i in range(size)])  9.15 us
    pallas_call x1, Pallas kernels, body(): pl.pallas_call(combine_kernel, out_shape=shape_of(every, deep, cols), in_...  5.17 us
    pallas_call x1, Pallas kernels, body(): pl.pallas_call(filter_kernel, out_shape=shape_of(groups, count, deep, col...  3.03 us
    pallas_call x1, Pallas kernels, body(): pl.pallas_call(lambda *refs: gram_kernel(1.0 / total, *refs), out_shape=s...  2.29 us
    pallas_call x1, Pallas kernels, body(): pl.pallas_call(edge_columns_kernel, out_shape=(shape_of(rows + 8, 128), s...  1.87 us
  transfers between devices with their start and end apart: 4, of which 2 were waited for; matrix products, arithmetic and copies ran while one was open for 0% of the time, Pallas kernels for 0%

profile of v1, /device:TPU:1, one launch (start us, length us, event | category | flops | bytes accessed | tf_op | source)
XLA Modules:
  0.0 87.6 jit_solution(3676905100729748229)
XLA Ops:
  0.0 1.8 %edge_rows.1 = (f32[64,512]{1,0:T(8,128)}, f32[16,512]{1,0:T(8,128)}, f32[16,512]{1,0:T(8,128)}) custom-call(f32[4,64,512]{2,1,0:T(8,128)} %v_ref.5, s32[64,512]{1,0:T(8,128)} %levels_ref.1, f32[8]{0:T(128)} %table_ref.1), custom_call_target="tpu_custom_call" | custom-call | tf_op jit(solution)/shard_map/edge_rows/pallas_call | solution.py:150
  1.8 2.1 %collective-permute-start = (f32[16,512]{1,0:T(8,128)}, f32[16,512]{1,0:T(8,128)S(1)}, u32[]{:S(2)}, u32[]{:S(2)}) collective-permute-start(f32[16,512]{1,0:T(8,128)} %get-tuple-element.11), channel_id=1, source_target_pairs={{0,8},{8,16},{16,24},{24,0},{1,9},{9,17},{17,25},{25,1},{2,10},{10... | collective-permute-start | bytes 98312 | tf_op jit(solution)/shard_map/ppermute | solution.py:136
  3.9 1.4 %collective-permute-start.1 = (f32[16,512]{1,0:T(8,128)}, f32[16,512]{1,0:T(8,128)S(1)}, u32[]{:S(2)}, u32[]{:S(2)}) collective-permute-start(f32[16,512]{1,0:T(8,128)} %get-tuple-element.12), channel_id=1, source_target_pairs={{0,24},{8,0},{16,8},{24,16},{1,25},{9,1},{17,9},{25,17},{2,26},{10... | collective-permute-start | bytes 98312 | tf_op jit(solution)/shard_map/ppermute | solution.py:136
  5.4 1.5 %collective-permute-done.above_ref = f32[16,512]{1,0:T(8,128)S(1)} collective-permute-done((f32[16,512]{1,0:T(8,128)}, f32[16,512]{1,0:T(8,128)S(1)}, u32[]{:S(2)}, u32[]{:S(2)}) %collective-permute-start) | collective-permute-done | bytes 32800 | tf_op jit(solution)/shard_map/ppermute | solution.py:136
  6.9 0.0 copy-start
  6.9 0.0 collective-permute-done.1.below_ref
  6.9 0.0 copy-start.1
  6.9 0.6 copy-done
  7.5 0.0 copy-done.1
  7.5 1.9 %edge_columns.1 = (f32[72,128]{1,0:T(8,128)}, f32[72,128]{1,0:T(8,128)}) custom-call(f32[4,64,512]{2,1,0:T(8,128)} %v_ref.5, f32[64,512]{1,0:T(8,128)} %get-tuple-element.10.onsite_ref, f32[16,512]{1,0:T(8,128)} %copy-done, f32[16,512]{1,0:T(8,128)} %copy-done.1), custom_call_target="tpu_custom_call" | custom-call | tf_op jit(solution)/shard_map/edge_columns/pallas_call | solution.py:159
  9.4 1.6 %collective-permute-start.2 = (f32[72,128]{1,0:T(8,128)}, f32[72,128]{1,0:T(8,128)S(1)}, u32[]{:S(2)}, u32[]{:S(2)}) collective-permute-start(f32[72,128]{1,0:T(8,128)} %get-tuple-element.13), channel_id=1, source_target_pairs={{0,1},{1,2},{2,3},{3,4},{4,5},{5,6},{6,7},{7,0},{8,9},{9,10},{10,1... | collective-permute-start | bytes 110600 | tf_op jit(solution)/shard_map/ppermute | solution.py:136
  11.0 3.9 %collective-permute-start.3 = (f32[72,128]{1,0:T(8,128)}, f32[72,128]{1,0:T(8,128)S(1)}, u32[]{:S(2)}, u32[]{:S(2)}) collective-permute-start(f32[72,128]{1,0:T(8,128)} %get-tuple-element.14), channel_id=1, source_target_pairs={{0,7},{1,0},{2,1},{3,2},{4,3},{5,4},{6,5},{7,6},{8,15},{9,8},{10,9... | collective-permute-start | bytes 110600 | tf_op jit(solution)/shard_map/ppermute | solution.py:136
  16.3 0.3 collective-permute-done.2.before_ref
  16.5 0.0 copy-start.2
  16.5 0.0 collective-permute-done.3.after_ref
  16.5 0.6 copy-done.2
  17.1 0.0 copy-start.3
  17.1 0.6 copy-done.3
  17.8 3.0 %filter.1 = f32[8,4,8,512]{3,2,1,0:T(8,128)} custom-call(f32[4,64,512]{2,1,0:T(8,128)} %v_ref.5, f32[64,512]{1,0:T(8,128)} %get-tuple-element.10.onsite_ref, f32[16,512]{1,0:T(8,128)} %copy-done, f32[16,512]{1,0:T(8,128)} %copy-done.1, f32[72,128]{1,0:T(8,128)} %copy-done.2, f32[72,128]{1,0:T(8,128)} %copy-done.3, f32[1]{0:T(128)S(6)} %copy.9.low_ref, ...), custom_call_target="tpu_custom_call" | custom-call | tf_op jit(solution)/shard_map/filter/pallas_call | solution.py:168
  20.8 16.7 %all_to_all.20 = f32[8,4,8,512]{3,2,1,0:T(8,128)} all-to-all(f32[8,4,8,512]{3,2,1,0:T(8,128)} %filter.1), channel_id=1, replica_groups=mesh['grp'=8,'lx'=4,'ly'=8] {'grp'}, dimensions={0} | all-to-all | bytes 1048576 | tf_op jit(solution)/shard_map/all_to_all | solution.py:175
  37.5 2.3 %gram.1 = f32[8,128]{1,0:T(8,128)} custom-call(f32[32,8,512]{2,1,0:T(8,128)} %bitcast.7), custom_call_target="tpu_custom_call" | custom-call | tf_op jit(solution)/shard_map/gram/pallas_call | solution.py:177
  39.8 0.7 broadcast_in_dim.4
  40.5 17.3 %all_to_all.21 = f32[32,8,128]{2,1,0:T(8,128)S(1)} all-to-all(f32[32,8,128]{2,1,0:T(8,128)S(1)} %broadcast_in_dim.4), channel_id=1, replica_groups=mesh['grp'=8,'lx'=4,'ly'=8] {'lx','ly'}, dimensions={0} | all-to-all | bytes 262144 | tf_op jit(solution)/shard_map/all_to_all | solution.py:141
  57.8 10.3 %all_to_all.22.gram_ref = f32[8,8,128]{2,1,0:T(8,128)} all-to-all(f32[8,8,128]{2,1,0:T(8,128)S(1)} %broadcast_in_dim.5), channel_id=1, replica_groups=mesh['grp'=8,'lx'=4,'ly'=8] {'grp'}, dimensions={0} | all-to-all | bytes 65536 | tf_op jit(solution)/shard_map/all_to_all | solution.py:141
  68.1 5.2 %combine.1 = f32[32,8,512]{2,1,0:T(8,128)} custom-call(f32[8,8,128]{2,1,0:T(8,128)} %all_to_all.22.gram_ref, f32[32,8,512]{2,1,0:T(8,128)} %bitcast.8), custom_call_target="tpu_custom_call" | custom-call | tf_op jit(solution)/shard_map/combine/pallas_call | solution.py:186
  73.2 13.5 %all_to_all.23 = f32[8,4,8,512]{3,2,1,0:T(8,128)S(1)} all-to-all(f32[8,4,8,512]{3,2,1,0:T(8,128)} %bitcast.9), channel_id=1, replica_groups=mesh['grp'=8,'lx'=4,'ly'=8] {'grp'}, dimensions={0} | all-to-all | bytes 1048576 | tf_op jit(solution)/shard_map/all_to_all | solution.py:193
  86.7 0.8 copy_bitcast_fusion
  (2 shorter events, 0.0 us)
Async XLA Ops:
  1.8 5.1 %collective-permute-start = (f32[16,512]{1,0:T(8,128)}, f32[16,512]{1,0:T(8,128)S(1)}, u32[]{:S(2)}, u32[]{:S(2)}) collective-permute-start(f32[16,512]{1,0:T(8,128)} %get-tuple-element.11), channel_id=1, source_target_pairs={{0,8},{8,16},{16,24},{24,0},{1,9},{9,17},{17,25},{25,1},{2,10},{10... | collective-permute-start | bytes 98312 | tf_op jit(solution)/shard_map/ppermute | solution.py:136
  3.9 3.0 %collective-permute-start.1 = (f32[16,512]{1,0:T(8,128)}, f32[16,512]{1,0:T(8,128)S(1)}, u32[]{:S(2)}, u32[]{:S(2)}) collective-permute-start(f32[16,512]{1,0:T(8,128)} %get-tuple-element.12), channel_id=1, source_target_pairs={{0,24},{8,0},{16,8},{24,16},{1,25},{9,1},{17,9},{25,17},{2,26},{10... | collective-permute-start | bytes 98312 | tf_op jit(solution)/shard_map/ppermute | solution.py:136
  6.9 0.6 copy-start
  6.9 0.6 copy-start.1
  9.4 7.1 %collective-permute-start.2 = (f32[72,128]{1,0:T(8,128)}, f32[72,128]{1,0:T(8,128)S(1)}, u32[]{:S(2)}, u32[]{:S(2)}) collective-permute-start(f32[72,128]{1,0:T(8,128)} %get-tuple-element.13), channel_id=1, source_target_pairs={{0,1},{1,2},{2,3},{3,4},{4,5},{5,6},{6,7},{7,0},{8,9},{9,10},{10,1... | collective-permute-start | bytes 110600 | tf_op jit(solution)/shard_map/ppermute | solution.py:136
  11.0 5.5 %collective-permute-start.3 = (f32[72,128]{1,0:T(8,128)}, f32[72,128]{1,0:T(8,128)S(1)}, u32[]{:S(2)}, u32[]{:S(2)}) collective-permute-start(f32[72,128]{1,0:T(8,128)} %get-tuple-element.14), channel_id=1, source_target_pairs={{0,7},{1,0},{2,1},{3,2},{4,3},{5,4},{6,5},{7,6},{8,15},{9,8},{10,9... | collective-permute-start | bytes 110600 | tf_op jit(solution)/shard_map/ppermute | solution.py:136
  16.5 0.6 copy-start.2
  17.1 0.6 copy-start.3

commit v2 on v1

v2 whole, which is shorter than its diff:
```python
import jax
import jax.numpy as jnp
from jax import lax
from jax.experimental import pallas as pl
from jax.experimental.pallas import tpu as pltpu
from jax.sharding import PartitionSpec as P

HIGHEST = lax.Precision.HIGHEST
VMEM = pl.BlockSpec(memory_space=pltpu.VMEM)
SMEM = pl.BlockSpec(memory_space=pltpu.SMEM)
COMPILER = pltpu.CompilerParams(vmem_limit_bytes=16 * 1024 * 1024)


def shape_of(*dims):
    return jax.ShapeDtypeStruct(dims, jnp.float32)


def vmem_shape_of(*dims):
    return pltpu.VMEM(dims, jnp.float32)


def onsite_of(levels, table_ref):
    onsite = jnp.zeros(levels.shape, jnp.float32)
    for k in range(table_ref.shape[0]):
        onsite = jnp.where(levels == k, table_ref[k], onsite)
    return onsite


def edge_rows_kernel(place_ref, top_ref, end_ref, top_levels_ref, end_levels_ref, table_ref, near_ref, far_ref):
    even = place_ref[1] == 0
    count, rows = top_ref.shape[0], top_ref.shape[1]
    top_onsite = onsite_of(top_levels_ref[...], table_ref)
    end_onsite = onsite_of(end_levels_ref[...], table_ref)
    for j in range(count + 1):
        first = top_ref[j, 0:2, :] if j < count else top_onsite[0:2]
        last = end_ref[j, rows - 2 : rows, :] if j < count else end_onsite[rows - 2 : rows]
        near_ref[2 * j : 2 * j + 2, :] = jnp.where(even, last, first)
        far_ref[2 * j : 2 * j + 2, :] = jnp.where(even, first, last)


def halo_rows(near_ref, far_ref, even, j, lanes):
    near, far = near_ref[2 * j : 2 * j + 2, lanes], far_ref[2 * j : 2 * j + 2, lanes]
    gap = jnp.zeros((4, lanes.stop - lanes.start), jnp.float32)
    return jnp.concatenate([jnp.where(even, near, far), gap, jnp.where(even, far, near)], axis=0)


def edge_columns_kernel(
    place_ref, left_ref, right_ref, left_levels_ref, right_levels_ref, table_ref, near_rows_ref, far_rows_ref, near_ref, far_ref
):
    even_row, even_col = place_ref[1] == 0, place_ref[2] == 0
    count, rows, _ = left_ref.shape
    cols = near_rows_ref.shape[1]
    lane = lax.broadcasted_iota(jnp.int32, (rows + 8, 128), 1)
    first = jnp.zeros((rows + 8, 128), jnp.float32)
    last = jnp.zeros((rows + 8, 128), jnp.float32)
    for j in range(count + 1):
        head, tail = slice(0, 128), slice(cols - 128, cols)
        own_head = left_ref[j] if j < count else onsite_of(left_levels_ref[...], table_ref)
        own_tail = right_ref[j] if j < count else onsite_of(right_levels_ref[...], table_ref)
        left = jnp.concatenate([own_head, halo_rows(near_rows_ref, far_rows_ref, even_row, j, head)], axis=0)
        right = jnp.concatenate([own_tail, halo_rows(near_rows_ref, far_rows_ref, even_row, j, tail)], axis=0)
        if j:
            left = pltpu.roll(left, 2 * j, 1)
            right = pltpu.roll(right, 128 - 2 * j, 1)
        first = jnp.where(lane // 2 == j, left, first)
        last = jnp.where((127 - lane) // 2 == j, right, last)
    near_ref[...] = jnp.where(even_col, last, first)
    far_ref[...] = jnp.where(even_col, first, last)


def filter_kernel(
    place_ref, v_ref, levels_ref, table_ref, near_rows_ref, far_rows_ref, near_ref, far_ref, low_ref, high_ref, out_ref
):
    even_row, even_col = place_ref[1] == 0, place_ref[2] == 0
    count, rows, cols = v_ref.shape
    strips = out_ref.shape[0]
    deep = rows // strips
    lane = lax.broadcasted_iota(jnp.int32, (rows + 8, 128), 1)
    wide = slice(0, cols)
    near, far = near_ref[...], far_ref[...]
    after = jnp.where(even_col, near, far)
    before = jnp.where(even_col, far, near)

    def extended(own, j):
        tall = jnp.concatenate([own, halo_rows(near_rows_ref, far_rows_ref, even_row, j, wide)], axis=0)
        right = pltpu.roll(after, 128 - 2 * j, 1) if j else after
        left = pltpu.roll(before, 2 * j, 1) if j else before
        return jnp.concatenate([tall, jnp.where(lane < 64, right, left)], axis=1)

    center = (high_ref[0] + low_ref[0]) / 2.0
    half = jnp.full((1, 1), (high_ref[0] - low_ref[0]) * 0.5, jnp.float32)
    scale = 1.0 / half
    weight = (extended(onsite_of(levels_ref[...], table_ref), count) - center) * scale

    def scaled_operator(x):
        height, width = x.shape
        beside = (pltpu.roll(x, 1, 0) + pltpu.roll(x, height - 1, 0)) + (
            pltpu.roll(x, 1, 1) + pltpu.roll(x, width - 1, 1)
        )
        return weight * x - scale * beside

    for j in range(count):
        x = extended(v_ref[j], j)
        filtered = 2.0 * scaled_operator(scaled_operator(x)) - x
        for s in range(strips):
            out_ref[s, j] = filtered[s * deep : (s + 1) * deep, :cols]


def gram_kernel(scale, x_ref, out_ref):
    count, deep, cols = x_ref.shape
    gram = jnp.zeros((count, 128), jnp.float32)
    none = jnp.zeros((128 - count, cols), jnp.float32)
    for r in range(deep):
        x = x_ref[:, r, :]
        gram = gram + lax.dot_general(
            x, jnp.concatenate([x, none], axis=0), (((1,), (1,)), ((), ())),
            precision=HIGHEST, preferred_element_type=jnp.float32,
        )
    packed = gram[0:8]
    for q in range(1, count // 8):
        packed = packed + pltpu.roll(gram[8 * q : 8 * q + 8], q * count, 1)
    out_ref[...] = jnp.broadcast_to((packed * scale)[None], out_ref.shape)


def factor_kernel(gram_ref, place_ref, factors_ref):
    count, every, _ = factors_ref.shape
    packed = gram_ref[0]
    for k in range(1, gram_ref.shape[0]):
        packed = packed + gram_ref[k]
    pieces = [packed] + [pltpu.roll(packed, 128 - q * every, 1) for q in range(1, every // 8)]
    row = lax.broadcasted_iota(jnp.int32, (every, 128), 0)
    lane = lax.broadcasted_iota(jnp.int32, (every, 128), 1)
    work = jnp.where(lane < every, jnp.concatenate(pieces, axis=0), 0.0)
    work = jnp.where(lane == row + every, 1.0, work)
    for j in range(every):
        pivot = work[j : j + 1, :]
        factor = work[:, j : j + 1] * (1.0 / work[j : j + 1, j : j + 1])
        work = work - jnp.where(row > j, factor, 0.0) * pivot
    diagonal = jnp.sum(jnp.where(lane == row, work, 0.0), axis=1, keepdims=True)
    inverse = work * (1.0 / jnp.sqrt(diagonal))
    for i in range(count):
        mine = jnp.sum(jnp.where(row == place_ref[0] * count + i, inverse, 0.0), axis=0, keepdims=True)
        upright = jnp.sum(jnp.where(lane == row + every, mine, 0.0), axis=1, keepdims=True)
        factors_ref[i] = jnp.broadcast_to(upright, (every, 128))


def combine_kernel(factors_ref, place_ref, *refs):
    *tiles, out_ref = refs
    strips, count, deep, cols = tiles[0].shape
    own = place_ref[0]

    def one_strip(s, carry):
        for c in range(cols // 128):
            lanes = slice(c * 128, c * 128 + 128)
            totals = [jnp.zeros((deep, 128), jnp.float32) for _ in range(count)]
            for q, tile in enumerate(tiles):
                first = (own ^ q) * count
                for k in range(count):
                    x = tile[s, k, :, lanes]
                    for i in range(count):
                        totals[i] = totals[i] + factors_ref[i, pl.ds(first + k, deep, stride=0), :] * x
            for i in range(count):
                out_ref[i, pl.ds(pl.multiple_of(s * deep, deep), deep), lanes] = totals[i]
        return carry

    lax.fori_loop(0, strips, one_strip, 0)


def swapped(value, axis, partner):
    return lax.ppermute(value, axis, [(i, partner(i)) for i in range(lax.axis_size(axis))])


def near_and_far(near, far, axis):
    size = lax.axis_size(axis)
    other = swapped(far, axis, lambda i: (i + (1 if i % 2 else -1)) % size)
    return swapped(near, axis, lambda i: i ^ 1), other


def in_vmem(*values):
    return [pltpu.with_memory_space_constraint(v, pltpu.VMEM) for v in values]


def body(vectors, levels, level_table, filter_low, filter_high):
    count, rows, cols = vectors.shape
    groups = lax.axis_size("grp")
    every = count * groups
    deep = rows // groups
    packed_rows = 8 * ((2 * (count + 1) + 7) // 8)
    place = jnp.stack([lax.axis_index("grp"), lax.axis_index("lx") % 2, lax.axis_index("ly") % 2])
    row_ends, col_ends = rows // 8 - 1, cols // 128 - 1
    hbm_vectors, hbm_levels = (pltpu.with_memory_space_constraint(v, pltpu.HBM) for v in (vectors, levels))
    near_rows, far_rows = pl.pallas_call(
        edge_rows_kernel,
        grid=(1,),
        out_shape=(vmem_shape_of(packed_rows, cols), vmem_shape_of(packed_rows, cols)),
        in_specs=[
            SMEM,
            pl.BlockSpec((count, 8, cols), lambda i: (0, 0, 0)),
            pl.BlockSpec((count, 8, cols), lambda i: (0, row_ends, 0)),
            pl.BlockSpec((8, cols), lambda i: (0, 0)),
            pl.BlockSpec((8, cols), lambda i: (row_ends, 0)),
            SMEM,
        ],
        out_specs=(VMEM, VMEM),
        compiler_params=COMPILER,
        name="edge_rows",
    )(place, hbm_vectors, hbm_vectors, hbm_levels, hbm_levels, level_table)
    near_rows, far_rows = in_vmem(*near_and_far(near_rows, far_rows, "lx"))
    near, far = pl.pallas_call(
        edge_columns_kernel,
        grid=(1,),
        out_shape=(vmem_shape_of(rows + 8, 128), vmem_shape_of(rows + 8, 128)),
        in_specs=[
            SMEM,
            pl.BlockSpec((count, rows, 128), lambda i: (0, 0, 0)),
            pl.BlockSpec((count, rows, 128), lambda i: (0, 0, col_ends)),
            pl.BlockSpec((rows, 128), lambda i: (0, 0)),
            pl.BlockSpec((rows, 128), lambda i: (0, col_ends)),
            SMEM,
            VMEM,
            VMEM,
        ],
        out_specs=(VMEM, VMEM),
        compiler_params=COMPILER,
        name="edge_columns",
    )(place, vectors, vectors, levels, levels, level_table, near_rows, far_rows)
    near, far = in_vmem(*near_and_far(near, far, "ly"))
    strips = pl.pallas_call(
        filter_kernel,
        out_shape=vmem_shape_of(groups, count, deep, cols),
        in_specs=[SMEM, VMEM, VMEM, SMEM] + [VMEM] * 4 + [SMEM] * 2,
        out_specs=VMEM,
        compiler_params=COMPILER,
        name="filter",
    )(place, vectors, levels, level_table, near_rows, far_rows, near, far, filter_low, filter_high)
    mine = lax.all_to_all(strips, "grp", 0, 0).reshape(every, deep, cols)
    strips, mine = lax.optimization_barrier((strips, mine))
    tiles = {0: strips, 1: swapped(strips, "grp", lambda i: i ^ 1)}
    for q in range(2, groups, 2):
        tiles[q] = swapped(strips, "grp", lambda i: i ^ q)
    planes = lax.axis_size("lx") * lax.axis_size("ly")
    total = rows * cols * planes
    gram = pl.pallas_call(
        lambda *refs: gram_kernel(1.0 / total, *refs),
        out_shape=vmem_shape_of(planes, 8, 128),
        in_specs=[VMEM],
        out_specs=VMEM,
        compiler_params=COMPILER,
        name="gram",
    )(*in_vmem(mine))
    gram = jnp.sum(lax.all_to_all(gram, ("lx", "ly"), 0, 0), axis=0)
    grams = lax.all_to_all(jnp.broadcast_to(gram[None], (groups,) + gram.shape), "grp", 0, 0)
    grams, tiles = lax.optimization_barrier((grams, tiles))
    for q in range(2, groups, 2):
        tiles[q + 1] = swapped(tiles[q], "grp", lambda i: i ^ 1)
    factors = pl.pallas_call(
        factor_kernel,
        out_shape=vmem_shape_of(count, every, 128),
        in_specs=[VMEM, SMEM],
        out_specs=VMEM,
        compiler_params=COMPILER,
        name="factor",
    )(*in_vmem(grams), place)
    return pl.pallas_call(
        combine_kernel,
        out_shape=shape_of(count, rows, cols),
        in_specs=[VMEM, SMEM] + [VMEM] * groups,
        out_specs=VMEM,
        compiler_params=COMPILER,
        name="combine",
    )(factors, place, *in_vmem(*[tiles[q] for q in range(groups)]))


def solution(mesh):
    in_specs = (P("grp", "lx", "ly"), P("lx", "ly"), P(), P(), P())
    out_specs = P("grp", "lx", "ly")
    return jax.shard_map(body, mesh=mesh, in_specs=in_specs, out_specs=out_specs, check_vma=False)
```

time: 88 us -> 74 us (0.84)
  blocking collectives: 57.7 us -> 42.4 us
  starting transfers between devices: 9.15 us -> 17 us
  Pallas kernels: 14.2 us -> 10.2 us
  local copies, waits for them, and re-layouts: 3.37 us -> 0.59 us
    all_to_all x3 -> x2, blocking collectives: 41 us -> 25.7 us  [the longest x1 16.5 us: body(): gram = jnp.sum(lax.all_to_all(gram, ('lx', 'ly'), 0, 0), axis=0)]
    ppermute x4 -> x11, starting transfers between devices: 9.15 us -> 17 us  [swapped(): lax.ppermute(value, axis, [(i, partner(i)) for i in range(lax.axis_size(a...]
    pallas_call x5 -> x6, Pallas kernels: 14.2 us -> 10.2 us  [the longest x1 3.27 us: body(): pl.pallas_call(factor_kernel, out_shape=vmem_shape_of(count, every, 128),...]
    unnamed x8 -> x6, local copies, waits for them, and re-layouts: 1.83 us -> 0.59 us
    ppermute x4 -> x11, waiting for transfers between devices: 1.79 us -> 2.15 us  [swapped(): lax.ppermute(value, axis, [(i, partner(i)) for i in range(lax.axis_size(a...]
  transfers between devices with their start and end apart: 4 -> 11, of which waited for: 2 -> 1; matrix products, arithmetic and copies ran while one was open for 0% -> 0% of each run, Pallas kernels for 0% -> 5%
where the time goes in v2:
time: 74 us; the launch traced here: 73.8 us
  blocking collectives  42.4 us (57%)
  starting transfers between devices  17 us (23%)
  Pallas kernels  10.2 us (14%)
  waiting for transfers between devices  2.15 us (3%)
  between operations  1.39 us (2%)
    ppermute x11, starting transfers between devices, swapped(): lax.ppermute(value, axis, [(i, partner(i)) for i in range(lax.axis_size(a...  17 us
    all_to_all x1, blocking collectives, body(): mine = lax.all_to_all(strips, 'grp', 0, 0).reshape(every, deep, cols)  16.7 us
    all_to_all x1, blocking collectives, body(): gram = jnp.sum(lax.all_to_all(gram, ('lx', 'ly'), 0, 0), axis=0)  16.5 us
    all_to_all x1, blocking collectives, body(): lax.all_to_all(jnp.broadcast_to(gram[None], (groups,) + gram.shape), 'grp...  9.15 us
    pallas_call x1, Pallas kernels, body(): pl.pallas_call(factor_kernel, out_shape=vmem_shape_of(count, every, 128),...  3.27 us
    pallas_call x1, Pallas kernels, body(): pl.pallas_call(combine_kernel, out_shape=shape_of(count, rows, cols), in_...  2.86 us
    ppermute x11, waiting for transfers between devices, swapped(): lax.ppermute(value, axis, [(i, partner(i)) for i in range(lax.axis_size(a...  2.15 us
    pallas_call x1, Pallas kernels, body(): pl.pallas_call(filter_kernel, out_shape=vmem_shape_of(groups, count, deep...  1.7 us
  transfers between devices with their start and end apart: 11, of which 1 were waited for; matrix products, arithmetic and copies ran while one was open for 0% of the time, Pallas kernels for 5%

profile of v2, /device:TPU:1, one launch (start us, length us, event | category | flops | bytes accessed | tf_op | source)
XLA Modules:
  0.0 73.8 jit_solution(2572877605556746642)
XLA Ops:
  0.0 0.0 copy-start.2
  0.0 0.1 pad_add_fusion.place_ref
  0.1 0.6 copy-done.2
  0.7 0.0 copy-start
  0.7 0.0 copy-start.1
  0.7 1.0 %edge_rows.1 = (f32[16,512]{1,0:T(8,128)S(1)}, f32[16,512]{1,0:T(8,128)S(1)}) custom-call(s32[3]{0:T(128)S(1)} %pad_add_fusion.place_ref, f32[4,64,512]{2,1,0:T(8,128)} %v_ref.1, f32[4,64,512]{2,1,0:T(8,128)} %v_ref.1, s32[64,512]{1,0:T(8,128)} %levels_ref.1, s32[64,512]{1,0:T(8,128)} %levels_ref.1, f32[8]{0:T(128)S(1)} %copy-done.2), custom_call_target="tpu_custom_call" | custom-call | tf_op jit(solution)/shard_map/edge_rows/pallas_call | solution.py:192
  1.7 2.2 %collective-permute-start = (f32[16,512]{1,0:T(8,128)S(1)}, f32[16,512]{1,0:T(8,128)S(1)}, u32[]{:S(2)}, u32[]{:S(2)}) collective-permute-start(f32[16,512]{1,0:T(8,128)S(1)} %get-tuple-element.17), channel_id=1, source_target_pairs={{0,8},{8,0},{16,24},{24,16},{1,9},{9,1},{17,25},{25,17},{2,10},{10... | collective-permute-start | bytes 98312 | tf_op jit(solution)/shard_map/ppermute | solution.py:170
  3.9 1.9 %collective-permute-start.1 = (f32[16,512]{1,0:T(8,128)S(1)}, f32[16,512]{1,0:T(8,128)S(1)}, u32[]{:S(2)}, u32[]{:S(2)}) collective-permute-start(f32[16,512]{1,0:T(8,128)S(1)} %get-tuple-element.18), channel_id=1, source_target_pairs={{0,24},{8,16},{16,8},{24,0},{1,25},{9,17},{17,9},{25,1},{2,26},{10... | collective-permute-start | bytes 98312 | tf_op jit(solution)/shard_map/ppermute | solution.py:170
  5.8 0.0 collective-permute-done.near_rows_ref
  5.8 2.1 %collective-permute-done.1.far_rows_ref = f32[16,512]{1,0:T(8,128)S(1)} collective-permute-done((f32[16,512]{1,0:T(8,128)S(1)}, f32[16,512]{1,0:T(8,128)S(1)}, u32[]{:S(2)}, u32[]{:S(2)}) %collective-permute-start.1) | collective-permute-done | bytes 32800 | tf_op jit(solution)/shard_map/ppermute | solution.py:170
  7.8 0.0 copy-done
  7.9 0.0 copy-done.1
  7.9 0.7 edge_columns.1
  8.5 1.7 %collective-permute-start.2 = (f32[72,128]{1,0:T(8,128)S(1)}, f32[72,128]{1,0:T(8,128)S(1)}, u32[]{:S(2)}, u32[]{:S(2)}) collective-permute-start(f32[72,128]{1,0:T(8,128)S(1)} %get-tuple-element.19), channel_id=1, source_target_pairs={{0,1},{1,0},{2,3},{3,2},{4,5},{5,4},{6,7},{7,6},{8,9},{9,8},{10,11... | collective-permute-start | bytes 110600 | tf_op jit(solution)/shard_map/ppermute | solution.py:170
  10.3 4.7 %collective-permute-start.3 = (f32[72,128]{1,0:T(8,128)S(1)}, f32[72,128]{1,0:T(8,128)S(1)}, u32[]{:S(2)}, u32[]{:S(2)}) collective-permute-start(f32[72,128]{1,0:T(8,128)S(1)} %get-tuple-element.20), channel_id=1, source_target_pairs={{0,7},{1,2},{2,1},{3,4},{4,3},{5,6},{6,5},{7,0},{8,15},{9,10},{10,... | collective-permute-start | bytes 110600 | tf_op jit(solution)/shard_map/ppermute | solution.py:170
  16.2 0.0 collective-permute-done.2.near_ref
  16.2 0.0 collective-permute-done.3.far_ref
  16.3 1.7 %filter.1.refs_0_ = f32[8,4,8,512]{3,2,1,0:T(8,128)S(1)} custom-call(s32[3]{0:T(128)S(1)} %pad_add_fusion.place_ref, f32[4,64,512]{2,1,0:T(8,128)S(1)} %copy-done, s32[64,512]{1,0:T(8,128)S(1)} %copy-done.1, f32[8]{0:T(128)S(1)} %copy-done.2, f32[16,512]{1,0:T(8,128)S(1)} %collective-permute-done.near_rows_ref, ...), custom_call_target="tpu_custom_call" | custom-call | tf_op jit(solution)/shard_map/filter/pallas_call | solution.py:228
  18.0 16.7 %all_to_all.15 = f32[8,4,8,512]{3,2,1,0:T(8,128)S(1)} all-to-all(f32[8,4,8,512]{3,2,1,0:T(8,128)S(1)} %filter.1.refs_0_), channel_id=1, replica_groups=mesh['grp'=8,'lx'=4,'ly'=8] {'grp'}, dimensions={0} | all-to-all | bytes 1048576 | tf_op jit(solution)/shard_map/all_to_all | solution.py:236
  34.7 0.9 %collective-permute-start.7 = (f32[8,4,8,512]{3,2,1,0:T(8,128)S(1)}, f32[8,4,8,512]{3,2,1,0:T(8,128)S(1)}, u32[]{:S(2)}, u32[]{:S(2)}) collective-permute-start(f32[8,4,8,512]{3,2,1,0:T(8,128)S(1)} %filter.1.refs_0_), channel_id=1, source_target_pairs={{0,192},{32,224},{64,128},{96,160},{128,64},{160,96},{192,0},{224,... | collective-permute-start | bytes 1572872 | tf_op jit(solution)/shard_map/ppermute | solution.py:170
  35.6 1.2 %collective-permute-start.6 = (f32[8,4,8,512]{3,2,1,0:T(8,128)S(1)}, f32[8,4,8,512]{3,2,1,0:T(8,128)S(1)}, u32[]{:S(2)}, u32[]{:S(2)}) collective-permute-start(f32[8,4,8,512]{3,2,1,0:T(8,128)S(1)} %filter.1.refs_0_), channel_id=1, source_target_pairs={{0,128},{32,160},{64,192},{96,224},{128,0},{160,32},{192,64},{224,... | collective-permute-start | bytes 1572872 | tf_op jit(solution)/shard_map/ppermute | solution.py:170
  36.8 1.2 %collective-permute-start.5 = (f32[8,4,8,512]{3,2,1,0:T(8,128)S(1)}, f32[8,4,8,512]{3,2,1,0:T(8,128)S(1)}, u32[]{:S(2)}, u32[]{:S(2)}) collective-permute-start(f32[8,4,8,512]{3,2,1,0:T(8,128)S(1)} %filter.1.refs_0_), channel_id=1, source_target_pairs={{0,64},{32,96},{64,0},{96,32},{128,192},{160,224},{192,128},{224,1... | collective-permute-start | bytes 1572872 | tf_op jit(solution)/shard_map/ppermute | solution.py:170
  38.0 1.9 %collective-permute-start.4 = (f32[8,4,8,512]{3,2,1,0:T(8,128)S(1)}, f32[8,4,8,512]{3,2,1,0:T(8,128)S(1)}, u32[]{:S(2)}, u32[]{:S(2)}) collective-permute-start(f32[8,4,8,512]{3,2,1,0:T(8,128)S(1)} %filter.1.refs_0_), channel_id=1, source_target_pairs={{0,32},{32,0},{64,96},{96,64},{128,160},{160,128},{192,224},{224,1... | collective-permute-start | bytes 1572872 | tf_op jit(solution)/shard_map/ppermute | solution.py:170
  39.8 0.7 gram.1
  40.5 16.5 %all_to_all.16 = f32[32,8,128]{2,1,0:T(8,128)S(1)} all-to-all(f32[32,8,128]{2,1,0:T(8,128)S(1)} %gram.1), channel_id=1, replica_groups=mesh['grp'=8,'lx'=4,'ly'=8] {'lx','ly'}, dimensions={0} | all-to-all | bytes 262144 | tf_op jit(solution)/shard_map/all_to_all | solution.py:251
  57.1 9.1 %all_to_all.17.gram_ref = f32[8,8,128]{2,1,0:T(8,128)S(1)} all-to-all(f32[8,8,128]{2,1,0:T(8,128)S(1)} %broadcast_in_dim.2), channel_id=1, replica_groups=mesh['grp'=8,'lx'=4,'ly'=8] {'grp'}, dimensions={0} | all-to-all | bytes 65536 | tf_op jit(solution)/shard_map/all_to_all | solution.py:252
  66.2 0.0 collective-permute-done.7.refs_6_
  66.2 0.0 collective-permute-done.6.refs_4_
  66.2 0.0 collective-permute-done.5.refs_2_
  66.2 0.0 collective-permute-done.4.refs_1_
  66.3 0.8 %collective-permute-start.8 = (f32[8,4,8,512]{3,2,1,0:T(8,128)S(1)}, f32[8,4,8,512]{3,2,1,0:T(8,128)S(1)}, u32[]{:S(2)}, u32[]{:S(2)}) collective-permute-start(f32[8,4,8,512]{3,2,1,0:T(8,128)S(1)} %collective-permute-done.5.refs_2_), channel_id=1, source_target_pairs={{0,32},{32,0},{64,96},{96,64},{128,160},{160,128},{192,224},{224,1... | collective-permute-start | bytes 1572872 | tf_op jit(solution)/shard_map/ppermute | solution.py:170
  67.1 0.1 collective-permute-start.9
  67.2 0.4 collective-permute-start.10
  67.6 3.3 %factor.1.factors_ref = f32[4,32,128]{2,1,0:T(8,128)S(1)} custom-call(f32[8,8,128]{2,1,0:T(8,128)S(1)} %all_to_all.17.gram_ref, s32[3]{0:T(128)S(1)} %pad_add_fusion.place_ref), custom_call_target="tpu_custom_call" | custom-call | tf_op jit(solution)/shard_map/factor/pallas_call | solution.py:256
  70.9 0.0 collective-permute-done.8.refs_3_
  70.9 0.0 collective-permute-done.9.refs_5_
  70.9 0.0 collective-permute-done.10.refs_7_
  70.9 2.9 %combine.1 = f32[4,64,512]{2,1,0:T(8,128)} custom-call(f32[4,32,128]{2,1,0:T(8,128)S(1)} %factor.1.factors_ref, s32[3]{0:T(128)S(1)} %pad_add_fusion.place_ref, f32[8,4,8,512]{3,2,1,0:T(8,128)S(1)} %filter.1.refs_0_, f32[8,4,8,512]{3,2,1,0:T(8,128)S(1)} %collective-permute-done.4.refs_1_, f32[8,4,8,512]{3,2,1,0:T(8,128)S(1)} %collective-permute-done.5.refs_2_, ...), custom_call_target="tpu_custom_call" | custom-call | tf_op jit(solution)/shard_map/combine/pallas_call | solution.py:264
  (2 shorter events, 0.0 us)
Async XLA Ops:
  0.0 0.7 copy-start.2
  0.7 7.2 %copy-start = (f32[4,64,512]{2,1,0:T(8,128)S(1)}, f32[4,64,512]{2,1,0:T(8,128)}, u32[]{:S(2)}) copy-start(f32[4,64,512]{2,1,0:T(8,128)} %v_ref.1) | copy-start | bytes 1572868
  0.7 7.2 %copy-start.1 = (s32[64,512]{1,0:T(8,128)S(1)}, s32[64,512]{1,0:T(8,128)}, u32[]{:S(2)}) copy-start(s32[64,512]{1,0:T(8,128)} %levels_ref.1) | copy-start | bytes 393220
  1.7 4.1 %collective-permute-start = (f32[16,512]{1,0:T(8,128)S(1)}, f32[16,512]{1,0:T(8,128)S(1)}, u32[]{:S(2)}, u32[]{:S(2)}) collective-permute-start(f32[16,512]{1,0:T(8,128)S(1)} %get-tuple-element.17), channel_id=1, source_target_pairs={{0,8},{8,0},{16,24},{24,16},{1,9},{9,1},{17,25},{25,17},{2,10},{10... | collective-permute-start | bytes 98312 | tf_op jit(solution)/shard_map/ppermute | solution.py:170
  3.9 4.0 %collective-permute-start.1 = (f32[16,512]{1,0:T(8,128)S(1)}, f32[16,512]{1,0:T(8,128)S(1)}, u32[]{:S(2)}, u32[]{:S(2)}) collective-permute-start(f32[16,512]{1,0:T(8,128)S(1)} %get-tuple-element.18), channel_id=1, source_target_pairs={{0,24},{8,16},{16,8},{24,0},{1,25},{9,17},{17,9},{25,1},{2,26},{10... | collective-permute-start | bytes 98312 | tf_op jit(solution)/shard_map/ppermute | solution.py:170
  8.5 7.7 %collective-permute-start.2 = (f32[72,128]{1,0:T(8,128)S(1)}, f32[72,128]{1,0:T(8,128)S(1)}, u32[]{:S(2)}, u32[]{:S(2)}) collective-permute-start(f32[72,128]{1,0:T(8,128)S(1)} %get-tuple-element.19), channel_id=1, source_target_pairs={{0,1},{1,0},{2,3},{3,2},{4,5},{5,4},{6,7},{7,6},{8,9},{9,8},{10,11... | collective-permute-start | bytes 110600 | tf_op jit(solution)/shard_map/ppermute | solution.py:170
  10.3 6.0 %collective-permute-start.3 = (f32[72,128]{1,0:T(8,128)S(1)}, f32[72,128]{1,0:T(8,128)S(1)}, u32[]{:S(2)}, u32[]{:S(2)}) collective-permute-start(f32[72,128]{1,0:T(8,128)S(1)} %get-tuple-element.20), channel_id=1, source_target_pairs={{0,7},{1,2},{2,1},{3,4},{4,3},{5,6},{6,5},{7,0},{8,15},{9,10},{10,... | collective-permute-start | bytes 110600 | tf_op jit(solution)/shard_map/ppermute | solution.py:170
  34.7 31.5 %collective-permute-start.7 = (f32[8,4,8,512]{3,2,1,0:T(8,128)S(1)}, f32[8,4,8,512]{3,2,1,0:T(8,128)S(1)}, u32[]{:S(2)}, u32[]{:S(2)}) collective-permute-start(f32[8,4,8,512]{3,2,1,0:T(8,128)S(1)} %filter.1.refs_0_), channel_id=1, source_target_pairs={{0,192},{32,224},{64,128},{96,160},{128,64},{160,96},{192,0},{224,... | collective-permute-start | bytes 1572872 | tf_op jit(solution)/shard_map/ppermute | solution.py:170
  35.6 30.7 %collective-permute-start.6 = (f32[8,4,8,512]{3,2,1,0:T(8,128)S(1)}, f32[8,4,8,512]{3,2,1,0:T(8,128)S(1)}, u32[]{:S(2)}, u32[]{:S(2)}) collective-permute-start(f32[8,4,8,512]{3,2,1,0:T(8,128)S(1)} %filter.1.refs_0_), channel_id=1, source_target_pairs={{0,128},{32,160},{64,192},{96,224},{128,0},{160,32},{192,64},{224,... | collective-permute-start | bytes 1572872 | tf_op jit(solution)/shard_map/ppermute | solution.py:170
  36.8 29.5 %collective-permute-start.5 = (f32[8,4,8,512]{3,2,1,0:T(8,128)S(1)}, f32[8,4,8,512]{3,2,1,0:T(8,128)S(1)}, u32[]{:S(2)}, u32[]{:S(2)}) collective-permute-start(f32[8,4,8,512]{3,2,1,0:T(8,128)S(1)} %filter.1.refs_0_), channel_id=1, source_target_pairs={{0,64},{32,96},{64,0},{96,32},{128,192},{160,224},{192,128},{224,1... | collective-permute-start | bytes 1572872 | tf_op jit(solution)/shard_map/ppermute | solution.py:170
  38.0 28.3 %collective-permute-start.4 = (f32[8,4,8,512]{3,2,1,0:T(8,128)S(1)}, f32[8,4,8,512]{3,2,1,0:T(8,128)S(1)}, u32[]{:S(2)}, u32[]{:S(2)}) collective-permute-start(f32[8,4,8,512]{3,2,1,0:T(8,128)S(1)} %filter.1.refs_0_), channel_id=1, source_target_pairs={{0,32},{32,0},{64,96},{96,64},{128,160},{160,128},{192,224},{224,1... | collective-permute-start | bytes 1572872 | tf_op jit(solution)/shard_map/ppermute | solution.py:170
  66.3 4.6 %collective-permute-start.8 = (f32[8,4,8,512]{3,2,1,0:T(8,128)S(1)}, f32[8,4,8,512]{3,2,1,0:T(8,128)S(1)}, u32[]{:S(2)}, u32[]{:S(2)}) collective-permute-start(f32[8,4,8,512]{3,2,1,0:T(8,128)S(1)} %collective-permute-done.5.refs_2_), channel_id=1, source_target_pairs={{0,32},{32,0},{64,96},{96,64},{128,160},{160,128},{192,224},{224,1... | collective-permute-start | bytes 1572872 | tf_op jit(solution)/shard_map/ppermute | solution.py:170
  67.1 3.8 %collective-permute-start.9 = (f32[8,4,8,512]{3,2,1,0:T(8,128)S(1)}, f32[8,4,8,512]{3,2,1,0:T(8,128)S(1)}, u32[]{:S(2)}, u32[]{:S(2)}) collective-permute-start(f32[8,4,8,512]{3,2,1,0:T(8,128)S(1)} %collective-permute-done.6.refs_4_), channel_id=1, source_target_pairs={{0,32},{32,0},{64,96},{96,64},{128,160},{160,128},{192,224},{224,1... | collective-permute-start | bytes 1572872 | tf_op jit(solution)/shard_map/ppermute | solution.py:170
  67.2 3.7 %collective-permute-start.10 = (f32[8,4,8,512]{3,2,1,0:T(8,128)S(1)}, f32[8,4,8,512]{3,2,1,0:T(8,128)S(1)}, u32[]{:S(2)}, u32[]{:S(2)}) collective-permute-start(f32[8,4,8,512]{3,2,1,0:T(8,128)S(1)} %collective-permute-done.7.refs_6_), channel_id=1, source_target_pairs={{0,32},{32,0},{64,96},{96,64},{128,160},{160,128},{192,224},{224,1... | collective-permute-start | bytes 1572872 | tf_op jit(solution)/shard_map/ppermute | solution.py:170

commit v3 on v2

--- a/solution.py
+++ b/solution.py
@@ -26,14 +26,14 @@
     return onsite
 
 
-def edge_rows_kernel(place_ref, top_ref, end_ref, top_levels_ref, end_levels_ref, table_ref, near_ref, far_ref):
+def edge_rows_kernel(place_ref, top_ref, end_ref, top_levels_ref, end_levels_ref, near_ref, far_ref):
     even = place_ref[1] == 0
     count, rows = top_ref.shape[0], top_ref.shape[1]
-    top_onsite = onsite_of(top_levels_ref[...], table_ref)
-    end_onsite = onsite_of(end_levels_ref[...], table_ref)
+    top_levels = top_levels_ref[...].astype(jnp.float32)
+    end_levels = end_levels_ref[...].astype(jnp.float32)
     for j in range(count + 1):
-        first = top_ref[j, 0:2, :] if j < count else top_onsite[0:2]
-        last = end_ref[j, rows - 2 : rows, :] if j < count else end_onsite[rows - 2 : rows]
+        first = top_ref[j, 0:2, :] if j < count else top_levels[0:2]
+        last = end_ref[j, rows - 2 : rows, :] if j < count else end_levels[rows - 2 : rows]
         near_ref[2 * j : 2 * j + 2, :] = jnp.where(even, last, first)
         far_ref[2 * j : 2 * j + 2, :] = jnp.where(even, first, last)
 
@@ -45,7 +45,7 @@
 
 
 def edge_columns_kernel(
-    place_ref, left_ref, right_ref, left_levels_ref, right_levels_ref, table_ref, near_rows_ref, far_rows_ref, near_ref, far_ref
+    place_ref, left_ref, right_ref, left_levels_ref, right_levels_ref, near_rows_ref, far_rows_ref, near_ref, far_ref
 ):
     even_row, even_col = place_ref[1] == 0, place_ref[2] == 0
     count, rows, _ = left_ref.shape
@@ -55,8 +55,8 @@
     last = jnp.zeros((rows + 8, 128), jnp.float32)
     for j in range(count + 1):
         head, tail = slice(0, 128), slice(cols - 128, cols)
-        own_head = left_ref[j] if j < count else onsite_of(left_levels_ref[...], table_ref)
-        own_tail = right_ref[j] if j < count else onsite_of(right_levels_ref[...], table_ref)
+        own_head = left_ref[j] if j < count else left_levels_ref[...].astype(jnp.float32)
+        own_tail = right_ref[j] if j < count else right_levels_ref[...].astype(jnp.float32)
         left = jnp.concatenate([own_head, halo_rows(near_rows_ref, far_rows_ref, even_row, j, head)], axis=0)
         right = jnp.concatenate([own_tail, halo_rows(near_rows_ref, far_rows_ref, even_row, j, tail)], axis=0)
         if j:
@@ -90,7 +90,7 @@
     center = (high_ref[0] + low_ref[0]) / 2.0
     half = jnp.full((1, 1), (high_ref[0] - low_ref[0]) * 0.5, jnp.float32)
     scale = 1.0 / half
-    weight = (extended(onsite_of(levels_ref[...], table_ref), count) - center) * scale
+    weight = (onsite_of(extended(levels_ref[...].astype(jnp.float32), count), table_ref) - center) * scale
 
     def scaled_operator(x):
         height, width = x.shape
@@ -122,6 +122,10 @@
     out_ref[...] = jnp.broadcast_to((packed * scale)[None], out_ref.shape)
 
 
+def spread_lane(x, j):
+    return jnp.broadcast_to(x[:, j : j + 1], x.shape)
+
+
 def factor_kernel(gram_ref, place_ref, factors_ref):
     count, every, _ = factors_ref.shape
     packed = gram_ref[0]
@@ -132,10 +136,15 @@
     lane = lax.broadcasted_iota(jnp.int32, (every, 128), 1)
     work = jnp.where(lane < every, jnp.concatenate(pieces, axis=0), 0.0)
     work = jnp.where(lane == row + every, 1.0, work)
-    for j in range(every):
-        pivot = work[j : j + 1, :]
-        factor = work[:, j : j + 1] * (1.0 / work[j : j + 1, j : j + 1])
-        work = work - jnp.where(row > j, factor, 0.0) * pivot
+    for j in range(0, every, 2):
+        top, next_row = work[j : j + 1, :], work[j + 1 : j + 2, :]
+        p, q, r = spread_lane(top, j), spread_lane(top, j + 1), spread_lane(next_row, j + 1)
+        inverse_p, inverse_det = 1.0 / p, 1.0 / (p * r - q * q)
+        first, second = (top * r - next_row * q) * inverse_det, (next_row * p - top * q) * inverse_det
+        left, right = spread_lane(work, j), spread_lane(work, j + 1)
+        below = row > j + 1
+        update = jnp.where(below, left, 0.0) * first + jnp.where(below, right, 0.0) * second
+        work = work - update - jnp.where(row == j + 1, left, 0.0) * (top * inverse_p)
     diagonal = jnp.sum(jnp.where(lane == row, work, 0.0), axis=1, keepdims=True)
     inverse = work * (1.0 / jnp.sqrt(diagonal))
     for i in range(count):
@@ -147,23 +156,25 @@
 def combine_kernel(factors_ref, place_ref, *refs):
     *tiles, out_ref = refs
     strips, count, deep, cols = tiles[0].shape
-    own = place_ref[0]
+    starts = [(place_ref[0] ^ q) * count for q in range(len(tiles))]
 
     def one_strip(s, carry):
-        for c in range(cols // 128):
-            lanes = slice(c * 128, c * 128 + 128)
-            totals = [jnp.zeros((deep, 128), jnp.float32) for _ in range(count)]
-            for q, tile in enumerate(tiles):
-                first = (own ^ q) * count
+        rows = pl.ds(pl.multiple_of(s * deep, deep), deep)
+        for c in range(0, cols, 256):
+            parts = [slice(c, c + 128), slice(c + 128, c + 256)]
+            totals = [[jnp.zeros((deep, 128), jnp.float32) for _ in parts] for _ in range(count)]
+            for start, tile in zip(starts, tiles):
                 for k in range(count):
-                    x = tile[s, k, :, lanes]
+                    fields = [tile[s, k, :, lanes] for lanes in parts]
                     for i in range(count):
-                        totals[i] = totals[i] + factors_ref[i, pl.ds(first + k, deep, stride=0), :] * x
+                        factor = factors_ref[i, pl.ds(start + k, deep, stride=0), :]
+                        totals[i] = [total + factor * field for total, field in zip(totals[i], fields)]
             for i in range(count):
-                out_ref[i, pl.ds(pl.multiple_of(s * deep, deep), deep), lanes] = totals[i]
+                for lanes, total in zip(parts, totals[i]):
+                    out_ref[i, rows, lanes] = total
         return carry
 
-    lax.fori_loop(0, strips, one_strip, 0)
+    lax.fori_loop(0, strips, one_strip, 0, unroll=True)
 
 
 def swapped(value, axis, partner):
@@ -172,8 +183,8 @@
 
 def near_and_far(near, far, axis):
     size = lax.axis_size(axis)
-    other = swapped(far, axis, lambda i: (i + (1 if i % 2 else -1)) % size)
-    return swapped(near, axis, lambda i: i ^ 1), other
+    near = swapped(near, axis, lambda i: i ^ 1)
+    return near, swapped(far, axis, lambda i: (i + (1 if i % 2 else -1)) % size)
 
 
 def in_vmem(*values):
@@ -199,12 +210,11 @@
             pl.BlockSpec((count, 8, cols), lambda i: (0, row_ends, 0)),
             pl.BlockSpec((8, cols), lambda i: (0, 0)),
             pl.BlockSpec((8, cols), lambda i: (row_ends, 0)),
-            SMEM,
         ],
         out_specs=(VMEM, VMEM),
         compiler_params=COMPILER,
         name="edge_rows",
-    )(place, hbm_vectors, hbm_vectors, hbm_levels, hbm_levels, level_table)
+    )(place, hbm_vectors, hbm_vectors, hbm_levels, hbm_levels)
     near_rows, far_rows = in_vmem(*near_and_far(near_rows, far_rows, "lx"))
     near, far = pl.pallas_call(
         edge_columns_kernel,
@@ -216,14 +226,13 @@
             pl.BlockSpec((count, rows, 128), lambda i: (0, 0, col_ends)),
             pl.BlockSpec((rows, 128), lambda i: (0, 0)),
             pl.BlockSpec((rows, 128), lambda i: (0, col_ends)),
-            SMEM,
             VMEM,
             VMEM,
         ],
         out_specs=(VMEM, VMEM),
         compiler_params=COMPILER,
         name="edge_columns",
-    )(place, vectors, vectors, levels, levels, level_table, near_rows, far_rows)
+    )(place, vectors, vectors, levels, levels, near_rows, far_rows)
     near, far = in_vmem(*near_and_far(near, far, "ly"))
     strips = pl.pallas_call(
         filter_kernel,
@@ -235,9 +244,8 @@
     )(place, vectors, levels, level_table, near_rows, far_rows, near, far, filter_low, filter_high)
     mine = lax.all_to_all(strips, "grp", 0, 0).reshape(every, deep, cols)
     strips, mine = lax.optimization_barrier((strips, mine))
-    tiles = {0: strips, 1: swapped(strips, "grp", lambda i: i ^ 1)}
-    for q in range(2, groups, 2):
-        tiles[q] = swapped(strips, "grp", lambda i: i ^ q)
+    tiles = {q: swapped(strips, "grp", lambda i, q=q: i ^ q) for q in (1, 4, 2, 6)}
+    tiles[0] = strips
     planes = lax.axis_size("lx") * lax.axis_size("ly")
     total = rows * cols * planes
     gram = pl.pallas_call(

time: 74 us -> 72.6 us (0.981)
  Pallas kernels: 10.2 us -> 8.99 us
    pallas_call x1, Pallas kernels: 3.27 us -> 2.17 us  [body(): pl.pallas_call(factor_kernel, out_shape=vmem_shape_of(count, every, 128),...]
  transfers between devices with their start and end apart: 11 -> 11, of which waited for: 1 -> 2; matrix products, arithmetic and copies ran while one was open for 0% -> 0% of each run, Pallas kernels for 5% -> 4%
where the time goes in v3:
time: 72.6 us; the launch traced here: 72.3 us
  blocking collectives  42.4 us (58%)
  starting transfers between devices  17 us (23%)
  Pallas kernels  8.99 us (12%)
  waiting for transfers between devices  2.44 us (3%)
  between operations  1.4 us (2%)
    ppermute x11, starting transfers between devices, swapped(): lax.ppermute(value, axis, [(i, partner(i)) for i in range(lax.axis_size(a...  17 us
    all_to_all x1, blocking collectives, body(): mine = lax.all_to_all(strips, 'grp', 0, 0).reshape(every, deep, cols)  16.7 us
    all_to_all x1, blocking collectives, body(): gram = jnp.sum(lax.all_to_all(gram, ('lx', 'ly'), 0, 0), axis=0)  16.5 us
    all_to_all x1, blocking collectives, body(): lax.all_to_all(jnp.broadcast_to(gram[None], (groups,) + gram.shape), 'grp...  9.15 us
    pallas_call x1, Pallas kernels, body(): pl.pallas_call(combine_kernel, out_shape=shape_of(count, rows, cols), in_...  2.76 us
    ppermute x11, waiting for transfers between devices, swapped(): lax.ppermute(value, axis, [(i, partner(i)) for i in range(lax.axis_size(a...  2.44 us
    pallas_call x1, Pallas kernels, body(): pl.pallas_call(factor_kernel, out_shape=vmem_shape_of(count, every, 128),...  2.17 us
    pallas_call x1, Pallas kernels, body(): pl.pallas_call(filter_kernel, out_shape=vmem_shape_of(groups, count, deep...  1.73 us
  transfers between devices with their start and end apart: 11, of which 2 were waited for; matrix products, arithmetic and copies ran while one was open for 0% of the time, Pallas kernels for 4%

profile of v3, /device:TPU:1, one launch (start us, length us, event | category | flops | bytes accessed | tf_op | source)
XLA Modules:
  0.0 72.3 jit_solution(8724342017413640821)
XLA Ops:
  0.0 0.1 pad_add_fusion.place_ref
  0.1 0.0 copy-start
  0.1 0.0 copy-start.1
  0.1 1.0 %edge_rows.1 = (f32[16,512]{1,0:T(8,128)S(1)}, f32[16,512]{1,0:T(8,128)S(1)}) custom-call(s32[3]{0:T(128)S(1)} %pad_add_fusion.place_ref, f32[4,64,512]{2,1,0:T(8,128)} %v_ref.1, f32[4,64,512]{2,1,0:T(8,128)} %v_ref.1, s32[64,512]{1,0:T(8,128)} %levels_ref.1, s32[64,512]{1,0:T(8,128)} %levels_ref.1), custom_call_target="tpu_custom_call" | custom-call | tf_op jit(solution)/shard_map/edge_rows/pallas_call | solution.py:203
  1.1 2.2 %collective-permute-start = (f32[16,512]{1,0:T(8,128)S(1)}, f32[16,512]{1,0:T(8,128)S(1)}, u32[]{:S(2)}, u32[]{:S(2)}) collective-permute-start(f32[16,512]{1,0:T(8,128)S(1)} %get-tuple-element.17), channel_id=1, source_target_pairs={{0,8},{8,0},{16,24},{24,16},{1,9},{9,1},{17,25},{25,17},{2,10},{10... | collective-permute-start | bytes 98312 | tf_op jit(solution)/shard_map/ppermute | solution.py:181
  3.3 1.9 %collective-permute-start.1 = (f32[16,512]{1,0:T(8,128)S(1)}, f32[16,512]{1,0:T(8,128)S(1)}, u32[]{:S(2)}, u32[]{:S(2)}) collective-permute-start(f32[16,512]{1,0:T(8,128)S(1)} %get-tuple-element.18), channel_id=1, source_target_pairs={{0,24},{8,16},{16,8},{24,0},{1,25},{9,17},{17,9},{25,1},{2,26},{10... | collective-permute-start | bytes 98312 | tf_op jit(solution)/shard_map/ppermute | solution.py:181
  5.2 0.0 collective-permute-done.near_rows_ref
  5.2 2.1 %collective-permute-done.1.far_rows_ref = f32[16,512]{1,0:T(8,128)S(1)} collective-permute-done((f32[16,512]{1,0:T(8,128)S(1)}, f32[16,512]{1,0:T(8,128)S(1)}, u32[]{:S(2)}, u32[]{:S(2)}) %collective-permute-start.1) | collective-permute-done | bytes 32800 | tf_op jit(solution)/shard_map/ppermute | solution.py:181
  7.2 0.0 copy-done
  7.3 0.0 copy-done.1
  7.3 0.7 edge_columns.1
  7.9 1.7 %collective-permute-start.2 = (f32[72,128]{1,0:T(8,128)S(1)}, f32[72,128]{1,0:T(8,128)S(1)}, u32[]{:S(2)}, u32[]{:S(2)}) collective-permute-start(f32[72,128]{1,0:T(8,128)S(1)} %get-tuple-element.19), channel_id=1, source_target_pairs={{0,1},{1,0},{2,3},{3,2},{4,5},{5,4},{6,7},{7,6},{8,9},{9,8},{10,11... | collective-permute-start | bytes 110600 | tf_op jit(solution)/shard_map/ppermute | solution.py:181
  9.7 4.7 %collective-permute-start.3 = (f32[72,128]{1,0:T(8,128)S(1)}, f32[72,128]{1,0:T(8,128)S(1)}, u32[]{:S(2)}, u32[]{:S(2)}) collective-permute-start(f32[72,128]{1,0:T(8,128)S(1)} %get-tuple-element.20), channel_id=1, source_target_pairs={{0,7},{1,2},{2,1},{3,4},{4,3},{5,6},{6,5},{7,0},{8,15},{9,10},{10,... | collective-permute-start | bytes 110600 | tf_op jit(solution)/shard_map/ppermute | solution.py:181
  15.0 0.0 copy-start.2
  15.7 0.0 collective-permute-done.2.near_ref
  15.7 0.0 collective-permute-done.3.far_ref
  15.7 0.0 copy-done.2
  15.7 1.7 %filter.1.refs_0_ = f32[8,4,8,512]{3,2,1,0:T(8,128)S(1)} custom-call(s32[3]{0:T(128)S(1)} %pad_add_fusion.place_ref, f32[4,64,512]{2,1,0:T(8,128)S(1)} %copy-done, s32[64,512]{1,0:T(8,128)S(1)} %copy-done.1, f32[8]{0:T(128)S(1)} %copy-done.2, f32[16,512]{1,0:T(8,128)S(1)} %collective-permute-done.near_rows_ref, ...), custom_call_target="tpu_custom_call" | custom-call | tf_op jit(solution)/shard_map/filter/pallas_call | solution.py:237
  17.4 16.7 %all_to_all.15 = f32[8,4,8,512]{3,2,1,0:T(8,128)S(1)} all-to-all(f32[8,4,8,512]{3,2,1,0:T(8,128)S(1)} %filter.1.refs_0_), channel_id=1, replica_groups=mesh['grp'=8,'lx'=4,'ly'=8] {'grp'}, dimensions={0} | all-to-all | bytes 1048576 | tf_op jit(solution)/shard_map/all_to_all | solution.py:245
  34.1 0.9 %collective-permute-start.7 = (f32[8,4,8,512]{3,2,1,0:T(8,128)S(1)}, f32[8,4,8,512]{3,2,1,0:T(8,128)S(1)}, u32[]{:S(2)}, u32[]{:S(2)}) collective-permute-start(f32[8,4,8,512]{3,2,1,0:T(8,128)S(1)} %filter.1.refs_0_), channel_id=1, source_target_pairs={{0,192},{32,224},{64,128},{96,160},{128,64},{160,96},{192,0},{224,... | collective-permute-start | bytes 1572872 | tf_op jit(solution)/shard_map/ppermute | solution.py:181
  35.0 1.2 %collective-permute-start.6 = (f32[8,4,8,512]{3,2,1,0:T(8,128)S(1)}, f32[8,4,8,512]{3,2,1,0:T(8,128)S(1)}, u32[]{:S(2)}, u32[]{:S(2)}) collective-permute-start(f32[8,4,8,512]{3,2,1,0:T(8,128)S(1)} %filter.1.refs_0_), channel_id=1, source_target_pairs={{0,128},{32,160},{64,192},{96,224},{128,0},{160,32},{192,64},{224,... | collective-permute-start | bytes 1572872 | tf_op jit(solution)/shard_map/ppermute | solution.py:181
  36.2 1.2 %collective-permute-start.5 = (f32[8,4,8,512]{3,2,1,0:T(8,128)S(1)}, f32[8,4,8,512]{3,2,1,0:T(8,128)S(1)}, u32[]{:S(2)}, u32[]{:S(2)}) collective-permute-start(f32[8,4,8,512]{3,2,1,0:T(8,128)S(1)} %filter.1.refs_0_), channel_id=1, source_target_pairs={{0,64},{32,96},{64,0},{96,32},{128,192},{160,224},{192,128},{224,1... | collective-permute-start | bytes 1572872 | tf_op jit(solution)/shard_map/ppermute | solution.py:181
  37.4 1.9 %collective-permute-start.4 = (f32[8,4,8,512]{3,2,1,0:T(8,128)S(1)}, f32[8,4,8,512]{3,2,1,0:T(8,128)S(1)}, u32[]{:S(2)}, u32[]{:S(2)}) collective-permute-start(f32[8,4,8,512]{3,2,1,0:T(8,128)S(1)} %filter.1.refs_0_), channel_id=1, source_target_pairs={{0,32},{32,0},{64,96},{96,64},{128,160},{160,128},{192,224},{224,1... | collective-permute-start | bytes 1572872 | tf_op jit(solution)/shard_map/ppermute | solution.py:181
  39.3 0.7 gram.1
  39.9 16.5 %all_to_all.16 = f32[32,8,128]{2,1,0:T(8,128)S(1)} all-to-all(f32[32,8,128]{2,1,0:T(8,128)S(1)} %gram.1), channel_id=1, replica_groups=mesh['grp'=8,'lx'=4,'ly'=8] {'lx','ly'}, dimensions={0} | all-to-all | bytes 262144 | tf_op jit(solution)/shard_map/all_to_all | solution.py:259
  56.5 9.1 %all_to_all.17.gram_ref = f32[8,8,128]{2,1,0:T(8,128)S(1)} all-to-all(f32[8,8,128]{2,1,0:T(8,128)S(1)} %broadcast_in_dim.2), channel_id=1, replica_groups=mesh['grp'=8,'lx'=4,'ly'=8] {'grp'}, dimensions={0} | all-to-all | bytes 65536 | tf_op jit(solution)/shard_map/all_to_all | solution.py:260
  65.7 0.0 collective-permute-done.7.refs_6_
  65.7 0.0 collective-permute-done.6.refs_4_
  65.7 0.0 collective-permute-done.5.refs_2_
  65.7 0.0 collective-permute-done.4.refs_1_
  65.7 0.8 %collective-permute-start.8 = (f32[8,4,8,512]{3,2,1,0:T(8,128)S(1)}, f32[8,4,8,512]{3,2,1,0:T(8,128)S(1)}, u32[]{:S(2)}, u32[]{:S(2)}) collective-permute-start(f32[8,4,8,512]{3,2,1,0:T(8,128)S(1)} %collective-permute-done.5.refs_2_), channel_id=1, source_target_pairs={{0,32},{32,0},{64,96},{96,64},{128,160},{160,128},{192,224},{224,1... | collective-permute-start | bytes 1572872 | tf_op jit(solution)/shard_map/ppermute | solution.py:181
  66.5 0.1 collective-permute-start.9
  66.6 0.4 collective-permute-start.10
  67.0 2.2 %factor.1.factors_ref = f32[4,32,128]{2,1,0:T(8,128)S(1)} custom-call(f32[8,8,128]{2,1,0:T(8,128)S(1)} %all_to_all.17.gram_ref, s32[3]{0:T(128)S(1)} %pad_add_fusion.place_ref), custom_call_target="tpu_custom_call" | custom-call | tf_op jit(solution)/shard_map/factor/pallas_call | solution.py:264
  69.2 0.0 collective-permute-done.8.refs_3_
  69.2 0.0 collective-permute-done.9.refs_5_
  69.2 0.3 collective-permute-done.10.refs_7_
  69.5 2.8 %combine.1 = f32[4,64,512]{2,1,0:T(8,128)} custom-call(f32[4,32,128]{2,1,0:T(8,128)S(1)} %factor.1.factors_ref, s32[3]{0:T(128)S(1)} %pad_add_fusion.place_ref, f32[8,4,8,512]{3,2,1,0:T(8,128)S(1)} %filter.1.refs_0_, f32[8,4,8,512]{3,2,1,0:T(8,128)S(1)} %collective-permute-done.4.refs_1_, f32[8,4,8,512]{3,2,1,0:T(8,128)S(1)} %collective-permute-done.5.refs_2_, ...), custom_call_target="tpu_custom_call" | custom-call | tf_op jit(solution)/shard_map/combine/pallas_call | solution.py:272
  (2 shorter events, 0.0 us)
Async XLA Ops:
  0.1 7.2 %copy-start = (f32[4,64,512]{2,1,0:T(8,128)S(1)}, f32[4,64,512]{2,1,0:T(8,128)}, u32[]{:S(2)}) copy-start(f32[4,64,512]{2,1,0:T(8,128)} %v_ref.1) | copy-start | bytes 1572868
  0.1 7.2 %copy-start.1 = (s32[64,512]{1,0:T(8,128)S(1)}, s32[64,512]{1,0:T(8,128)}, u32[]{:S(2)}) copy-start(s32[64,512]{1,0:T(8,128)} %levels_ref.1) | copy-start | bytes 393220
  1.1 4.1 %collective-permute-start = (f32[16,512]{1,0:T(8,128)S(1)}, f32[16,512]{1,0:T(8,128)S(1)}, u32[]{:S(2)}, u32[]{:S(2)}) collective-permute-start(f32[16,512]{1,0:T(8,128)S(1)} %get-tuple-element.17), channel_id=1, source_target_pairs={{0,8},{8,0},{16,24},{24,16},{1,9},{9,1},{17,25},{25,17},{2,10},{10... | collective-permute-start | bytes 98312 | tf_op jit(solution)/shard_map/ppermute | solution.py:181
  3.3 4.0 %collective-permute-start.1 = (f32[16,512]{1,0:T(8,128)S(1)}, f32[16,512]{1,0:T(8,128)S(1)}, u32[]{:S(2)}, u32[]{:S(2)}) collective-permute-start(f32[16,512]{1,0:T(8,128)S(1)} %get-tuple-element.18), channel_id=1, source_target_pairs={{0,24},{8,16},{16,8},{24,0},{1,25},{9,17},{17,9},{25,1},{2,26},{10... | collective-permute-start | bytes 98312 | tf_op jit(solution)/shard_map/ppermute | solution.py:181
  7.9 7.7 %collective-permute-start.2 = (f32[72,128]{1,0:T(8,128)S(1)}, f32[72,128]{1,0:T(8,128)S(1)}, u32[]{:S(2)}, u32[]{:S(2)}) collective-permute-start(f32[72,128]{1,0:T(8,128)S(1)} %get-tuple-element.19), channel_id=1, source_target_pairs={{0,1},{1,0},{2,3},{3,2},{4,5},{5,4},{6,7},{7,6},{8,9},{9,8},{10,11... | collective-permute-start | bytes 110600 | tf_op jit(solution)/shard_map/ppermute | solution.py:181
  9.7 6.0 %collective-permute-start.3 = (f32[72,128]{1,0:T(8,128)S(1)}, f32[72,128]{1,0:T(8,128)S(1)}, u32[]{:S(2)}, u32[]{:S(2)}) collective-permute-start(f32[72,128]{1,0:T(8,128)S(1)} %get-tuple-element.20), channel_id=1, source_target_pairs={{0,7},{1,2},{2,1},{3,4},{4,3},{5,6},{6,5},{7,0},{8,15},{9,10},{10,... | collective-permute-start | bytes 110600 | tf_op jit(solution)/shard_map/ppermute | solution.py:181
  15.0 0.7 copy-start.2
  34.1 31.5 %collective-permute-start.7 = (f32[8,4,8,512]{3,2,1,0:T(8,128)S(1)}, f32[8,4,8,512]{3,2,1,0:T(8,128)S(1)}, u32[]{:S(2)}, u32[]{:S(2)}) collective-permute-start(f32[8,4,8,512]{3,2,1,0:T(8,128)S(1)} %filter.1.refs_0_), channel_id=1, source_target_pairs={{0,192},{32,224},{64,128},{96,160},{128,64},{160,96},{192,0},{224,... | collective-permute-start | bytes 1572872 | tf_op jit(solution)/shard_map/ppermute | solution.py:181
  35.0 30.7 %collective-permute-start.6 = (f32[8,4,8,512]{3,2,1,0:T(8,128)S(1)}, f32[8,4,8,512]{3,2,1,0:T(8,128)S(1)}, u32[]{:S(2)}, u32[]{:S(2)}) collective-permute-start(f32[8,4,8,512]{3,2,1,0:T(8,128)S(1)} %filter.1.refs_0_), channel_id=1, source_target_pairs={{0,128},{32,160},{64,192},{96,224},{128,0},{160,32},{192,64},{224,... | collective-permute-start | bytes 1572872 | tf_op jit(solution)/shard_map/ppermute | solution.py:181
  36.2 29.5 %collective-permute-start.5 = (f32[8,4,8,512]{3,2,1,0:T(8,128)S(1)}, f32[8,4,8,512]{3,2,1,0:T(8,128)S(1)}, u32[]{:S(2)}, u32[]{:S(2)}) collective-permute-start(f32[8,4,8,512]{3,2,1,0:T(8,128)S(1)} %filter.1.refs_0_), channel_id=1, source_target_pairs={{0,64},{32,96},{64,0},{96,32},{128,192},{160,224},{192,128},{224,1... | collective-permute-start | bytes 1572872 | tf_op jit(solution)/shard_map/ppermute | solution.py:181
  37.4 28.3 %collective-permute-start.4 = (f32[8,4,8,512]{3,2,1,0:T(8,128)S(1)}, f32[8,4,8,512]{3,2,1,0:T(8,128)S(1)}, u32[]{:S(2)}, u32[]{:S(2)}) collective-permute-start(f32[8,4,8,512]{3,2,1,0:T(8,128)S(1)} %filter.1.refs_0_), channel_id=1, source_target_pairs={{0,32},{32,0},{64,96},{96,64},{128,160},{160,128},{192,224},{224,1... | collective-permute-start | bytes 1572872 | tf_op jit(solution)/shard_map/ppermute | solution.py:181
  65.7 3.5 %collective-permute-start.8 = (f32[8,4,8,512]{3,2,1,0:T(8,128)S(1)}, f32[8,4,8,512]{3,2,1,0:T(8,128)S(1)}, u32[]{:S(2)}, u32[]{:S(2)}) collective-permute-start(f32[8,4,8,512]{3,2,1,0:T(8,128)S(1)} %collective-permute-done.5.refs_2_), channel_id=1, source_target_pairs={{0,32},{32,0},{64,96},{96,64},{128,160},{160,128},{192,224},{224,1... | collective-permute-start | bytes 1572872 | tf_op jit(solution)/shard_map/ppermute | solution.py:181
  66.5 2.7 %collective-permute-start.9 = (f32[8,4,8,512]{3,2,1,0:T(8,128)S(1)}, f32[8,4,8,512]{3,2,1,0:T(8,128)S(1)}, u32[]{:S(2)}, u32[]{:S(2)}) collective-permute-start(f32[8,4,8,512]{3,2,1,0:T(8,128)S(1)} %collective-permute-done.6.refs_4_), channel_id=1, source_target_pairs={{0,32},{32,0},{64,96},{96,64},{128,160},{160,128},{192,224},{224,1... | collective-permute-start | bytes 1572872 | tf_op jit(solution)/shard_map/ppermute | solution.py:181
  66.6 2.9 %collective-permute-start.10 = (f32[8,4,8,512]{3,2,1,0:T(8,128)S(1)}, f32[8,4,8,512]{3,2,1,0:T(8,128)S(1)}, u32[]{:S(2)}, u32[]{:S(2)}) collective-permute-start(f32[8,4,8,512]{3,2,1,0:T(8,128)S(1)} %collective-permute-done.7.refs_6_), channel_id=1, source_target_pairs={{0,32},{32,0},{64,96},{96,64},{128,160},{160,128},{192,224},{224,1... | collective-permute-start | bytes 1572872 | tf_op jit(solution)/shard_map/ppermute | solution.py:181

commit v4 on v3

v4 whole, which is shorter than its diff:
```python
import jax
import jax.numpy as jnp
from jax import lax
from jax.experimental import pallas as pl
from jax.experimental.pallas import tpu as pltpu
from jax.sharding import PartitionSpec as P

HIGHEST = lax.Precision.HIGHEST
VMEM = pl.BlockSpec(memory_space=pltpu.VMEM)
SMEM = pl.BlockSpec(memory_space=pltpu.SMEM)
COMPILER = pltpu.CompilerParams(vmem_limit_bytes=16 * 1024 * 1024)


def shape_of(*dims):
    return jax.ShapeDtypeStruct(dims, jnp.float32)


def vmem_shape_of(*dims):
    return pltpu.VMEM(dims, jnp.float32)


def onsite_of(levels, table_ref):
    onsite = jnp.zeros(levels.shape, jnp.float32)
    for k in range(table_ref.shape[0]):
        onsite = jnp.where(levels == k, table_ref[k], onsite)
    return onsite


def halo_rows(near_ref, far_ref, even, j, parts, chosen):
    tiles = []
    for c in chosen:
        at = 2 * (j * parts + c)
        near, far = near_ref[at : at + 2, :], far_ref[at : at + 2, :]
        tiles.append(
            jnp.concatenate(
                [jnp.where(even, near, far), jnp.zeros((4, 128), jnp.float32), jnp.where(even, far, near)], axis=0
            )
        )
    return jnp.concatenate(tiles, axis=1)


def packed_lanes(x):
    groups = x.shape[0] // 8
    blocks = []
    for start in range(0, groups, 8):
        block = x[8 * start : 8 * start + 8]
        for t in range(1, min(8, groups - start)):
            block = block + pltpu.roll(x[8 * (start + t) : 8 * (start + t) + 8], 16 * t, 1)
        blocks.append(block)
    return jnp.concatenate(blocks, axis=1)


def unpacked_lanes(x, groups):
    tiles = []
    for t in range(groups):
        block = x[:, 128 * (t // 8) : 128 * (t // 8) + 128]
        tiles.append(pltpu.roll(block, 128 - 16 * (t % 8), 1) if t % 8 else block)
    return jnp.concatenate(tiles, axis=0)


def edges_kernel(
    place_ref, top_ref, end_ref, left_ref, right_ref, top_levels_ref, end_levels_ref, left_levels_ref, right_levels_ref,
    near_rows_ref, far_rows_ref, near_cols_ref, far_cols_ref,
):
    even_row, even_col = place_ref[1] == 0, place_ref[2] == 0
    count, deep = top_ref.shape[0], top_ref.shape[1]
    parts = top_ref.shape[2] // 128
    top_levels = top_levels_ref[...].astype(jnp.float32)
    end_levels = end_levels_ref[...].astype(jnp.float32)
    for j in range(count + 1):
        first = top_ref[j, 0:2, :] if j < count else top_levels[0:2]
        last = end_ref[j, deep - 2 : deep, :] if j < count else end_levels[deep - 2 : deep]
        near, far = jnp.where(even_row, last, first), jnp.where(even_row, first, last)
        for c in range(parts):
            at = 2 * (j * parts + c)
            near_rows_ref[at : at + 2, :] = near[:, c * 128 : c * 128 + 128]
            far_rows_ref[at : at + 2, :] = far[:, c * 128 : c * 128 + 128]
    rows = left_ref.shape[1]
    lane = lax.broadcasted_iota(jnp.int32, (rows, 128), 1)
    first = jnp.zeros((rows, 128), jnp.float32)
    last = jnp.zeros((rows, 128), jnp.float32)
    for j in range(count + 1):
        left = left_ref[j] if j < count else left_levels_ref[...].astype(jnp.float32)
        right = right_ref[j] if j < count else right_levels_ref[...].astype(jnp.float32)
        if j:
            left = pltpu.roll(left, 2 * j, 1)
            right = pltpu.roll(right, 128 - 2 * j, 1)
        first = jnp.where(lane // 2 == j, left, first)
        last = jnp.where((127 - lane) // 2 == j, right, last)
    first, last = packed_lanes(first), packed_lanes(last)
    near_cols_ref[...] = jnp.where(even_col, last, first)
    far_cols_ref[...] = jnp.where(even_col, first, last)


def filter_kernel(
    place_ref, v_ref, levels_ref, table_ref, near_rows_ref, far_rows_ref, near_ref, far_ref, low_ref, high_ref, out_ref, corner_ref
):
    even_row, even_col = place_ref[1] == 0, place_ref[2] == 0
    count, rows, cols = v_ref.shape
    strips = out_ref.shape[0]
    deep = rows // strips
    lane = lax.broadcasted_iota(jnp.int32, (rows, 128), 1)
    parts = cols // 128
    near, far = near_ref[...], far_ref[...]
    after = unpacked_lanes(jnp.where(even_col, near, far), rows // 8)
    before = unpacked_lanes(jnp.where(even_col, far, near), rows // 8)

    def extended(own, j):
        tall = jnp.concatenate([own, halo_rows(near_rows_ref, far_rows_ref, even_row, j, parts, range(parts))], axis=0)
        right = pltpu.roll(after, 128 - 2 * j, 1) if j else after
        left = pltpu.roll(before, 2 * j, 1) if j else before
        side = jnp.concatenate([jnp.where(lane < 64, right, left), jnp.zeros((8, 128), jnp.float32)], axis=0)
        return jnp.concatenate([tall, side], axis=1)

    center = (high_ref[0] + low_ref[0]) / 2.0
    half = jnp.full((1, 1), (high_ref[0] - low_ref[0]) * 0.5, jnp.float32)
    scale = 1.0 / half
    weight = (onsite_of(extended(levels_ref[...].astype(jnp.float32), count), table_ref) - center) * scale

    def scaled_operator(x):
        height, width = x.shape
        beside = (pltpu.roll(x, 1, 0) + pltpu.roll(x, height - 1, 0)) + (
            pltpu.roll(x, 1, 1) + pltpu.roll(x, width - 1, 1)
        )
        return weight * x - scale * beside

    site = lax.broadcasted_iota(jnp.int32, (1, 128), 1)
    row_at = lax.broadcasted_iota(jnp.int32, (rows, cols), 0)
    col_at = lax.broadcasted_iota(jnp.int32, (rows, cols), 1)
    inside = ((row_at > 0) & (row_at < rows - 1)) | ((col_at > 0) & (col_at < cols - 1))
    corners = [(0, 0), (0, cols - 1), (rows - 1, 0), (rows - 1, cols - 1)]
    corner_ref[...] = jnp.zeros(corner_ref.shape, jnp.float32)
    for j in range(count):
        own = v_ref[j]
        x = extended(own, j)
        filtered = (2.0 * scaled_operator(scaled_operator(x)) - x)[:rows, :cols]
        held = jnp.zeros((1, 128), jnp.float32)
        for c, (r, l) in enumerate(corners):
            held = held + jnp.where(site == place_ref[3] + c, filtered[r : r + 1, l : l + 1], 0.0)
            held = held + jnp.where(site == place_ref[4 + c], 4.0 * scale * scale * own[r : r + 1, l : l + 1], 0.0)
        corner_ref[j : j + 1, :] = held
        filtered = jnp.where(inside, filtered, 0.0)
        for s in range(strips):
            out_ref[s, j] = filtered[s * deep : (s + 1) * deep]


def gram_kernel(scale, x_ref, corner_ref, out_ref):
    count, deep, cols = x_ref.shape
    gram = jnp.zeros((count, 128), jnp.float32)
    none = jnp.zeros((128 - count, cols), jnp.float32)
    for r in range(deep):
        x = x_ref[:, r, :]
        gram = gram + lax.dot_general(
            x, jnp.concatenate([x, none], axis=0), (((1,), (1,)), ((), ())),
            precision=HIGHEST, preferred_element_type=jnp.float32,
        )
    packed = gram[0:8]
    for q in range(1, count // 8):
        packed = packed + pltpu.roll(gram[8 * q : 8 * q + 8], q * count, 1)
    both = jnp.concatenate([packed * scale, corner_ref[0 : out_ref.shape[1] - 8, :]], axis=0)
    out_ref[...] = jnp.broadcast_to(both[None], out_ref.shape)


def spread_lane(x, j):
    return jnp.broadcast_to(x[:, j : j + 1], x.shape)


def factor_kernel(scale, gram_ref, place_ref, factors_ref, corners_ref):
    count, every, _ = factors_ref.shape
    packed = gram_ref[0, 0:8, :]
    for k in range(1, gram_ref.shape[0]):
        packed = packed + gram_ref[k, 0:8, :]
    sites = jnp.concatenate([gram_ref[k, 8 : 8 + count, :] for k in range(gram_ref.shape[0])], axis=0)
    none = jnp.zeros((128 - every, 128), jnp.float32)
    at_corners = lax.dot_general(
        sites, jnp.concatenate([sites, none], axis=0), (((1,), (1,)), ((), ())),
        precision=HIGHEST, preferred_element_type=jnp.float32,
    )
    pieces = [packed] + [pltpu.roll(packed, 128 - q * every, 1) for q in range(1, every // 8)]
    row = lax.broadcasted_iota(jnp.int32, (every, 128), 0)
    lane = lax.broadcasted_iota(jnp.int32, (every, 128), 1)
    work = jnp.where(lane < every, jnp.concatenate(pieces, axis=0) + at_corners * scale, 0.0)
    work = jnp.where(lane == row + every, 1.0, work)
    for j in range(0, every, 2):
        top, next_row = work[j : j + 1, :], work[j + 1 : j + 2, :]
        p, q, r = spread_lane(top, j), spread_lane(top, j + 1), spread_lane(next_row, j + 1)
        inverse_p, inverse_det = 1.0 / p, 1.0 / (p * r - q * q)
        first, second = (top * r - next_row * q) * inverse_det, (next_row * p - top * q) * inverse_det
        left, right = spread_lane(work, j), spread_lane(work, j + 1)
        below = row > j + 1
        update = jnp.where(below, left, 0.0) * first + jnp.where(below, right, 0.0) * second
        work = work - update - jnp.where(row == j + 1, left, 0.0) * (top * inverse_p)
    diagonal = jnp.sum(jnp.where(lane == row, work, 0.0), axis=1, keepdims=True)
    inverse = work * (1.0 / jnp.sqrt(diagonal))
    for i in range(count):
        mine = jnp.sum(jnp.where(row == place_ref[0] * count + i, inverse, 0.0), axis=0, keepdims=True)
        upright = jnp.sum(jnp.where(lane == row + every, mine, 0.0), axis=1, keepdims=True)
        factors_ref[i] = jnp.broadcast_to(upright, (every, 128))
        basis = jnp.sum(upright * sites, axis=0, keepdims=True)
        for c in range(4):
            value = jnp.sum(jnp.where(lane[0:1] == place_ref[3] + c, basis, 0.0), axis=1, keepdims=True)
            corners_ref[4 * i + c : 4 * i + c + 1, :] = jnp.where(lane[0:1] == (127 if c % 2 else 0), value, 0.0)


def combine_kernel(factors_ref, corners_ref, place_ref, *refs):
    *tiles, out_ref = refs
    strips, count, deep, cols = tiles[0].shape
    starts = [(place_ref[0] ^ q) * count for q in range(len(tiles))]

    def one_strip(s, carry):
        rows = pl.ds(pl.multiple_of(s * deep, deep), deep)
        for c in range(0, cols, 256):
            parts = [slice(c, c + 128), slice(c + 128, c + 256)]
            totals = [[jnp.zeros((deep, 128), jnp.float32) for _ in parts] for _ in range(count)]
            for start, tile in zip(starts, tiles):
                for k in range(count):
                    fields = [tile[s, k, :, lanes] for lanes in parts]
                    for i in range(count):
                        factor = factors_ref[i, pl.ds(start + k, deep, stride=0), :]
                        totals[i] = [total + factor * field for total, field in zip(totals[i], fields)]
            for i in range(count):
                for lanes, total in zip(parts, totals[i]):
                    out_ref[i, rows, lanes] = total
        return carry

    lax.fori_loop(0, strips, one_strip, 0, unroll=True)
    last = strips * deep - 1
    for i in range(count):
        for c, (row, first) in enumerate([(0, 0), (0, cols - 128), (last, 0), (last, cols - 128)]):
            at = (slice(row, row + 1), slice(first, first + 128))
            out_ref[i, *at] = out_ref[i, *at] + corners_ref[4 * i + c : 4 * i + c + 1, :]


def swapped(value, axis, partner):
    return lax.ppermute(value, axis, [(i, partner(i)) for i in range(lax.axis_size(axis))])


def near_and_far(near, far, axis):
    size = lax.axis_size(axis)
    near = swapped(near, axis, lambda i: i ^ 1)
    return near, swapped(far, axis, lambda i: (i + (1 if i % 2 else -1)) % size)


def in_vmem(*values):
    return [pltpu.with_memory_space_constraint(v, pltpu.VMEM) for v in values]


def body(vectors, levels, level_table, filter_low, filter_high):
    count, rows, cols = vectors.shape
    groups = lax.axis_size("grp")
    every = count * groups
    deep = rows // groups
    packed_rows = 2 * (count + 1) * (cols // 128)
    here_x, here_y = lax.axis_index("lx"), lax.axis_index("ly")
    size_x, size_y = lax.axis_size("lx"), lax.axis_size("ly")
    beyond = [
        4 * ((here_x + dx) % size_x * size_y + (here_y + dy) % size_y) + 3 - c
        for c, (dx, dy) in enumerate([(-1, -1), (-1, 1), (1, -1), (1, 1)])
    ]
    place = jnp.stack([lax.axis_index("grp"), here_x % 2, here_y % 2, 4 * (here_x * size_y + here_y), *beyond])
    row_ends, col_ends = rows // 8 - 1, cols // 128 - 1
    hbm_vectors, hbm_levels = (pltpu.with_memory_space_constraint(v, pltpu.HBM) for v in (vectors, levels))
    near_rows, far_rows, near, far = pl.pallas_call(
        edges_kernel,
        grid=(1,),
        out_shape=(vmem_shape_of(packed_rows, 128),) * 2 + (vmem_shape_of(8, 128),) * 2,
        in_specs=[
            SMEM,
            pl.BlockSpec((count, 8, cols), lambda i: (0, 0, 0)),
            pl.BlockSpec((count, 8, cols), lambda i: (0, row_ends, 0)),
            pl.BlockSpec((count, rows, 128), lambda i: (0, 0, 0)),
            pl.BlockSpec((count, rows, 128), lambda i: (0, 0, col_ends)),
            pl.BlockSpec((8, cols), lambda i: (0, 0)),
            pl.BlockSpec((8, cols), lambda i: (row_ends, 0)),
            pl.BlockSpec((rows, 128), lambda i: (0, 0)),
            pl.BlockSpec((rows, 128), lambda i: (0, col_ends)),
        ],
        out_specs=(VMEM,) * 4,
        compiler_params=COMPILER,
        name="edges",
    )(place, *[hbm_vectors] * 4, *[hbm_levels] * 4)
    near_rows, far_rows = in_vmem(*near_and_far(near_rows, far_rows, "lx"))
    near, far = in_vmem(*near_and_far(near, far, "ly"))
    strips, corner = pl.pallas_call(
        filter_kernel,
        out_shape=(vmem_shape_of(groups, count, deep, cols), vmem_shape_of(8, 128)),
        in_specs=[SMEM, VMEM, VMEM, SMEM] + [VMEM] * 4 + [SMEM] * 2,
        out_specs=(VMEM, VMEM),
        compiler_params=COMPILER,
        name="filter",
    )(place, vectors, levels, level_table, near_rows, far_rows, near, far, filter_low, filter_high)
    mine = lax.all_to_all(strips, "grp", 0, 0).reshape(every, deep, cols)
    strips, mine = lax.optimization_barrier((strips, mine))
    tiles = {q: swapped(strips, "grp", lambda i, q=q: i ^ q) for q in (1, 4, 2, 6)}
    tiles[0] = strips
    planes = lax.axis_size("lx") * lax.axis_size("ly")
    total = rows * cols * planes
    gram = pl.pallas_call(
        lambda *refs: gram_kernel(1.0 / total, *refs),
        out_shape=vmem_shape_of(planes, 8 + count, 128),
        in_specs=[VMEM, VMEM],
        out_specs=VMEM,
        compiler_params=COMPILER,
        name="gram",
    )(*in_vmem(mine), corner)
    gram = jnp.sum(lax.all_to_all(gram, ("lx", "ly"), 0, 0), axis=0)
    grams = lax.all_to_all(jnp.broadcast_to(gram[None], (groups,) + gram.shape), "grp", 0, 0)
    grams, tiles = lax.optimization_barrier((grams, tiles))
    for q in range(2, groups, 2):
        tiles[q + 1] = swapped(tiles[q], "grp", lambda i: i ^ 1)
    factors, corners = pl.pallas_call(
        lambda *refs: factor_kernel(1.0 / total, *refs),
        out_shape=(vmem_shape_of(count, every, 128), vmem_shape_of(4 * count, 128)),
        in_specs=[VMEM, SMEM],
        out_specs=(VMEM, VMEM),
        compiler_params=COMPILER,
        name="factor",
    )(*in_vmem(grams), place)
    return pl.pallas_call(
        combine_kernel,
        out_shape=shape_of(count, rows, cols),
        in_specs=[VMEM, VMEM, SMEM] + [VMEM] * groups,
        out_specs=VMEM,
        compiler_params=COMPILER,
        name="combine",
    )(factors, corners, place, *in_vmem(*[tiles[q] for q in range(groups)]))


def solution(mesh):
    in_specs = (P("grp", "lx", "ly"), P("lx", "ly"), P(), P(), P())
    out_specs = P("grp", "lx", "ly")
    return jax.shard_map(body, mesh=mesh, in_specs=in_specs, out_specs=out_specs, check_vma=False)
```

time: 72.6 us -> 69.4 us (0.956)
  waiting for transfers between devices: 2.44 us -> 0.1 us
  blocking collectives: 42.4 us -> 41.6 us
    ppermute x11, waiting for transfers between devices: 2.44 us -> 0.1 us  [swapped(): lax.ppermute(value, axis, [(i, partner(i)) for i in range(lax.axis_size(a...]
    all_to_all x1, blocking collectives: 16.7 us -> 15.5 us  [body(): mine = lax.all_to_all(strips, 'grp', 0, 0).reshape(every, deep, cols)]
    pallas_call x4 -> x3, Pallas kernels: 5.55 us -> 5.79 us  [the longest x1 2.42 us: body(): pl.pallas_call(lambda *refs: factor_kernel(1.0 / total, *refs), out_shape...]
  transfers between devices with their start and end apart: 11 -> 11, of which waited for: 2 -> 1; matrix products, arithmetic and copies ran while one was open for 0% -> 0% of each run, Pallas kernels for 4% -> 4%
where the time goes in v4:
time: 69.4 us; the launch traced here: 69.2 us
  blocking collectives  41.6 us (60%)
  starting transfers between devices  16.9 us (24%)
  Pallas kernels  8.98 us (13%)
  between operations  1.44 us (2%)
    ppermute x11, starting transfers between devices, swapped(): lax.ppermute(value, axis, [(i, partner(i)) for i in range(lax.axis_size(a...  16.9 us
    all_to_all x1, blocking collectives, body(): gram = jnp.sum(lax.all_to_all(gram, ('lx', 'ly'), 0, 0), axis=0)  16.6 us
    all_to_all x1, blocking collectives, body(): mine = lax.all_to_all(strips, 'grp', 0, 0).reshape(every, deep, cols)  15.5 us
    all_to_all x1, blocking collectives, body(): lax.all_to_all(jnp.broadcast_to(gram[None], (groups,) + gram.shape), 'grp...  9.55 us
    pallas_call x1, Pallas kernels, body(): pl.pallas_call(combine_kernel, out_shape=shape_of(count, rows, cols), in_...  2.51 us
    pallas_call x1, Pallas kernels, body(): pl.pallas_call(lambda *refs: factor_kernel(1.0 / total, *refs), out_shape...  2.42 us
    pallas_call x1, Pallas kernels, body(): pl.pallas_call(filter_kernel, out_shape=(vmem_shape_of(groups, count, dee...  2.04 us
  transfers between devices with their start and end apart: 11, of which 1 were waited for; matrix products, arithmetic and copies ran while one was open for 0% of the time, Pallas kernels for 4%

profile of v4, /device:TPU:1, one launch (start us, length us, event | category | flops | bytes accessed | tf_op | source)
XLA Modules:
  0.0 69.2 jit_solution(17116378646528233805)
XLA Ops:
  0.0 0.1 stack.35.place_ref.refs_1_
  0.1 0.0 copy-start
  0.1 0.0 copy-start.1
  0.1 1.3 %edges.1 = (f32[40,128]{1,0:T(8,128)S(1)}, f32[40,128]{1,0:T(8,128)S(1)}, f32[8,128]{1,0:T(8,128)S(1)}, f32[8,128]{1,0:T(8,128)S(1)}) custom-call(s32[8]{0:T(128)S(1)} %stack.35.place_ref.refs_1_, f32[4,64,512]{2,1,0:T(8,128)} %v_ref.1, f32[4,64,512]{2,1,0:T(8,128)} %v_ref.1, f32[4,64,512]{2,1,0:T(8,128)} %v_ref.1, f32[4,64,512]{2,1,0:T(8,128)} %v_ref.1, ...), custom_call_target="tpu_custom_call" | custom-call | tf_op jit(solution)/shard_map/edges/pallas_call | solution.py:263
  1.4 2.2 %collective-permute-start = (f32[40,128]{1,0:T(8,128)S(1)}, f32[40,128]{1,0:T(8,128)S(1)}, u32[]{:S(2)}, u32[]{:S(2)}) collective-permute-start(f32[40,128]{1,0:T(8,128)S(1)} %get-tuple-element.21), channel_id=1, source_target_pairs={{0,8},{8,0},{16,24},{24,16},{1,9},{9,1},{17,25},{25,17},{2,10},{10... | collective-permute-start | bytes 61448 | tf_op jit(solution)/shard_map/ppermute | solution.py:235
  3.6 1.9 %collective-permute-start.1 = (f32[40,128]{1,0:T(8,128)S(1)}, f32[40,128]{1,0:T(8,128)S(1)}, u32[]{:S(2)}, u32[]{:S(2)}) collective-permute-start(f32[40,128]{1,0:T(8,128)S(1)} %get-tuple-element.22), channel_id=1, source_target_pairs={{0,24},{8,16},{16,8},{24,0},{1,25},{9,17},{17,9},{25,1},{2,26},{10... | collective-permute-start | bytes 61448 | tf_op jit(solution)/shard_map/ppermute | solution.py:235
  5.5 1.6 %collective-permute-start.2 = (f32[8,128]{1,0:T(8,128)S(1)}, f32[8,128]{1,0:T(8,128)S(1)}, u32[]{:S(2)}, u32[]{:S(2)}) collective-permute-start(f32[8,128]{1,0:T(8,128)S(1)} %get-tuple-element.23), channel_id=1, source_target_pairs={{0,1},{1,0},{2,3},{3,2},{4,5},{5,4},{6,7},{7,6},{8,9},{9,8},{10,11... | collective-permute-start | bytes 12296 | tf_op jit(solution)/shard_map/ppermute | solution.py:235
  7.2 4.7 %collective-permute-start.3 = (f32[8,128]{1,0:T(8,128)S(1)}, f32[8,128]{1,0:T(8,128)S(1)}, u32[]{:S(2)}, u32[]{:S(2)}) collective-permute-start(f32[8,128]{1,0:T(8,128)S(1)} %get-tuple-element.24), channel_id=1, source_target_pairs={{0,7},{1,2},{2,1},{3,4},{4,3},{5,6},{6,5},{7,0},{8,15},{9,10},{10,... | collective-permute-start | bytes 12296 | tf_op jit(solution)/shard_map/ppermute | solution.py:235
  12.5 0.0 copy-start.2
  13.2 0.0 collective-permute-done.2.near_ref
  13.2 0.0 collective-permute-done.3.far_ref
  13.2 0.0 collective-permute-done.near_rows_ref
  13.2 0.0 collective-permute-done.1.far_rows_ref
  13.2 0.0 copy-done
  13.2 0.0 copy-done.1
  13.2 0.0 copy-done.2
  13.2 2.0 %filter.1 = (f32[8,4,8,512]{3,2,1,0:T(8,128)S(1)}, f32[8,128]{1,0:T(8,128)S(1)}) custom-call(s32[8]{0:T(128)S(1)} %stack.35.place_ref.refs_1_, f32[4,64,512]{2,1,0:T(8,128)S(1)} %copy-done, s32[64,512]{1,0:T(8,128)S(1)} %copy-done.1, f32[8]{0:T(128)S(1)} %copy-done.2, f32[40,128]{1,0:T(8,128)S(1)} %collective-permute-done.near_rows_ref, ...), custom_call_target="tpu_custom_call" | custom-call | tf_op jit(solution)/shard_map/filter/pallas_call | solution.py:284
  15.3 15.5 %all_to_all.15 = f32[8,4,8,512]{3,2,1,0:T(8,128)S(1)} all-to-all(f32[8,4,8,512]{3,2,1,0:T(8,128)S(1)} %get-tuple-element.32.refs_0_), channel_id=1, replica_groups=mesh['grp'=8,'lx'=4,'ly'=8] {'grp'}, dimensions={0} | all-to-all | bytes 1048576 | tf_op jit(solution)/shard_map/all_to_all | solution.py:292
  30.8 0.9 %collective-permute-start.7 = (f32[8,4,8,512]{3,2,1,0:T(8,128)S(1)}, f32[8,4,8,512]{3,2,1,0:T(8,128)S(1)}, u32[]{:S(2)}, u32[]{:S(2)}) collective-permute-start(f32[8,4,8,512]{3,2,1,0:T(8,128)S(1)} %get-tuple-element.32.refs_0_), channel_id=1, source_target_pairs={{0,192},{32,224},{64,128},{96,160},{128,64},{160,96},{192,0},{224,... | collective-permute-start | bytes 1572872 | tf_op jit(solution)/shard_map/ppermute | solution.py:235
  31.6 1.2 %collective-permute-start.6 = (f32[8,4,8,512]{3,2,1,0:T(8,128)S(1)}, f32[8,4,8,512]{3,2,1,0:T(8,128)S(1)}, u32[]{:S(2)}, u32[]{:S(2)}) collective-permute-start(f32[8,4,8,512]{3,2,1,0:T(8,128)S(1)} %get-tuple-element.32.refs_0_), channel_id=1, source_target_pairs={{0,128},{32,160},{64,192},{96,224},{128,0},{160,32},{192,64},{224,... | collective-permute-start | bytes 1572872 | tf_op jit(solution)/shard_map/ppermute | solution.py:235
  32.8 1.2 %collective-permute-start.5 = (f32[8,4,8,512]{3,2,1,0:T(8,128)S(1)}, f32[8,4,8,512]{3,2,1,0:T(8,128)S(1)}, u32[]{:S(2)}, u32[]{:S(2)}) collective-permute-start(f32[8,4,8,512]{3,2,1,0:T(8,128)S(1)} %get-tuple-element.32.refs_0_), channel_id=1, source_target_pairs={{0,64},{32,96},{64,0},{96,32},{128,192},{160,224},{192,128},{224,1... | collective-permute-start | bytes 1572872 | tf_op jit(solution)/shard_map/ppermute | solution.py:235
  34.0 1.9 %collective-permute-start.4 = (f32[8,4,8,512]{3,2,1,0:T(8,128)S(1)}, f32[8,4,8,512]{3,2,1,0:T(8,128)S(1)}, u32[]{:S(2)}, u32[]{:S(2)}) collective-permute-start(f32[8,4,8,512]{3,2,1,0:T(8,128)S(1)} %get-tuple-element.32.refs_0_), channel_id=1, source_target_pairs={{0,32},{32,0},{64,96},{96,64},{128,160},{160,128},{192,224},{224,1... | collective-permute-start | bytes 1572872 | tf_op jit(solution)/shard_map/ppermute | solution.py:235
  35.9 0.7 gram.1
  36.6 16.6 %all_to_all.16 = f32[32,12,128]{2,1,0:T(8,128)S(1)} all-to-all(f32[32,12,128]{2,1,0:T(8,128)S(1)} %gram.1), channel_id=1, replica_groups=mesh['grp'=8,'lx'=4,'ly'=8] {'lx','ly'}, dimensions={0} | all-to-all | bytes 393216 | tf_op jit(solution)/shard_map/all_to_all | solution.py:306
  53.2 9.5 %all_to_all.17.refs_0_ = f32[8,12,128]{2,1,0:T(8,128)S(1)} all-to-all(f32[8,12,128]{2,1,0:T(8,128)S(1)} %broadcast_in_dim.2), channel_id=1, replica_groups=mesh['grp'=8,'lx'=4,'ly'=8] {'grp'}, dimensions={0} | all-to-all | bytes 98304 | tf_op jit(solution)/shard_map/all_to_all | solution.py:307
  62.7 0.0 collective-permute-done.7.refs_6_
  62.7 0.0 collective-permute-done.6.refs_4_
  62.7 0.0 collective-permute-done.5.refs_2_
  62.8 0.0 collective-permute-done.4.refs_1_
  62.8 0.9 %collective-permute-start.8 = (f32[8,4,8,512]{3,2,1,0:T(8,128)S(1)}, f32[8,4,8,512]{3,2,1,0:T(8,128)S(1)}, u32[]{:S(2)}, u32[]{:S(2)}) collective-permute-start(f32[8,4,8,512]{3,2,1,0:T(8,128)S(1)} %collective-permute-done.5.refs_2_), channel_id=1, source_target_pairs={{0,32},{32,0},{64,96},{96,64},{128,160},{160,128},{192,224},{224,1... | collective-permute-start | bytes 1572872 | tf_op jit(solution)/shard_map/ppermute | solution.py:235
  63.6 0.1 collective-permute-start.9
  63.7 0.4 collective-permute-start.10
  64.1 2.4 %factor.1 = (f32[4,32,128]{2,1,0:T(8,128)S(1)}, f32[16,128]{1,0:T(8,128)S(1)}) custom-call(f32[8,12,128]{2,1,0:T(8,128)S(1)} %all_to_all.17.refs_0_, s32[8]{0:T(128)S(1)} %stack.35.place_ref.refs_1_), custom_call_target="tpu_custom_call" | custom-call | tf_op jit(solution)/shard_map/factor/pallas_call | solution.py:311
  66.6 0.0 collective-permute-done.8.refs_3_
  66.6 0.0 collective-permute-done.9.refs_5_
  66.6 0.1 collective-permute-done.10.refs_7_
  66.7 2.5 %combine.1 = f32[4,64,512]{2,1,0:T(8,128)} custom-call(f32[4,32,128]{2,1,0:T(8,128)S(1)} %get-tuple-element.30.factors_ref, f32[16,128]{1,0:T(8,128)S(1)} %get-tuple-element.31.corners_ref, s32[8]{0:T(128)S(1)} %stack.35.place_ref.refs_1_, f32[8,4,8,512]{3,2,1,0:T(8,128)S(1)} %get-tuple-element.32.refs_0_, ...), custom_call_target="tpu_custom_call" | custom-call | tf_op jit(solution)/shard_map/combine/pallas_call | solution.py:319
  (2 shorter events, 0.0 us)
Async XLA Ops:
  0.1 13.1 %copy-start = (f32[4,64,512]{2,1,0:T(8,128)S(1)}, f32[4,64,512]{2,1,0:T(8,128)}, u32[]{:S(2)}) copy-start(f32[4,64,512]{2,1,0:T(8,128)} %v_ref.1) | copy-start | bytes 1572868
  0.1 13.1 %copy-start.1 = (s32[64,512]{1,0:T(8,128)S(1)}, s32[64,512]{1,0:T(8,128)}, u32[]{:S(2)}) copy-start(s32[64,512]{1,0:T(8,128)} %levels_ref.1) | copy-start | bytes 393220
  1.4 11.8 %collective-permute-start = (f32[40,128]{1,0:T(8,128)S(1)}, f32[40,128]{1,0:T(8,128)S(1)}, u32[]{:S(2)}, u32[]{:S(2)}) collective-permute-start(f32[40,128]{1,0:T(8,128)S(1)} %get-tuple-element.21), channel_id=1, source_target_pairs={{0,8},{8,0},{16,24},{24,16},{1,9},{9,1},{17,25},{25,17},{2,10},{10... | collective-permute-start | bytes 61448 | tf_op jit(solution)/shard_map/ppermute | solution.py:235
  3.6 9.6 %collective-permute-start.1 = (f32[40,128]{1,0:T(8,128)S(1)}, f32[40,128]{1,0:T(8,128)S(1)}, u32[]{:S(2)}, u32[]{:S(2)}) collective-permute-start(f32[40,128]{1,0:T(8,128)S(1)} %get-tuple-element.22), channel_id=1, source_target_pairs={{0,24},{8,16},{16,8},{24,0},{1,25},{9,17},{17,9},{25,1},{2,26},{10... | collective-permute-start | bytes 61448 | tf_op jit(solution)/shard_map/ppermute | solution.py:235
  5.5 7.6 %collective-permute-start.2 = (f32[8,128]{1,0:T(8,128)S(1)}, f32[8,128]{1,0:T(8,128)S(1)}, u32[]{:S(2)}, u32[]{:S(2)}) collective-permute-start(f32[8,128]{1,0:T(8,128)S(1)} %get-tuple-element.23), channel_id=1, source_target_pairs={{0,1},{1,0},{2,3},{3,2},{4,5},{5,4},{6,7},{7,6},{8,9},{9,8},{10,11... | collective-permute-start | bytes 12296 | tf_op jit(solution)/shard_map/ppermute | solution.py:235
  7.2 6.0 %collective-permute-start.3 = (f32[8,128]{1,0:T(8,128)S(1)}, f32[8,128]{1,0:T(8,128)S(1)}, u32[]{:S(2)}, u32[]{:S(2)}) collective-permute-start(f32[8,128]{1,0:T(8,128)S(1)} %get-tuple-element.24), channel_id=1, source_target_pairs={{0,7},{1,2},{2,1},{3,4},{4,3},{5,6},{6,5},{7,0},{8,15},{9,10},{10,... | collective-permute-start | bytes 12296 | tf_op jit(solution)/shard_map/ppermute | solution.py:235
  12.5 0.7 %copy-start.2 = (f32[8]{0:T(128)S(1)}, f32[8]{0:T(128)}, u32[]{:S(2)}) copy-start(f32[8]{0:T(128)} %table_ref.1) | copy-start | bytes 100
  30.8 32.0 %collective-permute-start.7 = (f32[8,4,8,512]{3,2,1,0:T(8,128)S(1)}, f32[8,4,8,512]{3,2,1,0:T(8,128)S(1)}, u32[]{:S(2)}, u32[]{:S(2)}) collective-permute-start(f32[8,4,8,512]{3,2,1,0:T(8,128)S(1)} %get-tuple-element.32.refs_0_), channel_id=1, source_target_pairs={{0,192},{32,224},{64,128},{96,160},{128,64},{160,96},{192,0},{224,... | collective-permute-start | bytes 1572872 | tf_op jit(solution)/shard_map/ppermute | solution.py:235
  31.6 31.1 %collective-permute-start.6 = (f32[8,4,8,512]{3,2,1,0:T(8,128)S(1)}, f32[8,4,8,512]{3,2,1,0:T(8,128)S(1)}, u32[]{:S(2)}, u32[]{:S(2)}) collective-permute-start(f32[8,4,8,512]{3,2,1,0:T(8,128)S(1)} %get-tuple-element.32.refs_0_), channel_id=1, source_target_pairs={{0,128},{32,160},{64,192},{96,224},{128,0},{160,32},{192,64},{224,... | collective-permute-start | bytes 1572872 | tf_op jit(solution)/shard_map/ppermute | solution.py:235
  32.8 29.9 %collective-permute-start.5 = (f32[8,4,8,512]{3,2,1,0:T(8,128)S(1)}, f32[8,4,8,512]{3,2,1,0:T(8,128)S(1)}, u32[]{:S(2)}, u32[]{:S(2)}) collective-permute-start(f32[8,4,8,512]{3,2,1,0:T(8,128)S(1)} %get-tuple-element.32.refs_0_), channel_id=1, source_target_pairs={{0,64},{32,96},{64,0},{96,32},{128,192},{160,224},{192,128},{224,1... | collective-permute-start | bytes 1572872 | tf_op jit(solution)/shard_map/ppermute | solution.py:235
  34.0 28.7 %collective-permute-start.4 = (f32[8,4,8,512]{3,2,1,0:T(8,128)S(1)}, f32[8,4,8,512]{3,2,1,0:T(8,128)S(1)}, u32[]{:S(2)}, u32[]{:S(2)}) collective-permute-start(f32[8,4,8,512]{3,2,1,0:T(8,128)S(1)} %get-tuple-element.32.refs_0_), channel_id=1, source_target_pairs={{0,32},{32,0},{64,96},{96,64},{128,160},{160,128},{192,224},{224,1... | collective-permute-start | bytes 1572872 | tf_op jit(solution)/shard_map/ppermute | solution.py:235
  62.8 3.8 %collective-permute-start.8 = (f32[8,4,8,512]{3,2,1,0:T(8,128)S(1)}, f32[8,4,8,512]{3,2,1,0:T(8,128)S(1)}, u32[]{:S(2)}, u32[]{:S(2)}) collective-permute-start(f32[8,4,8,512]{3,2,1,0:T(8,128)S(1)} %collective-permute-done.5.refs_2_), channel_id=1, source_target_pairs={{0,32},{32,0},{64,96},{96,64},{128,160},{160,128},{192,224},{224,1... | collective-permute-start | bytes 1572872 | tf_op jit(solution)/shard_map/ppermute | solution.py:235
  63.6 3.0 %collective-permute-start.9 = (f32[8,4,8,512]{3,2,1,0:T(8,128)S(1)}, f32[8,4,8,512]{3,2,1,0:T(8,128)S(1)}, u32[]{:S(2)}, u32[]{:S(2)}) collective-permute-start(f32[8,4,8,512]{3,2,1,0:T(8,128)S(1)} %collective-permute-done.6.refs_4_), channel_id=1, source_target_pairs={{0,32},{32,0},{64,96},{96,64},{128,160},{160,128},{192,224},{224,1... | collective-permute-start | bytes 1572872 | tf_op jit(solution)/shard_map/ppermute | solution.py:235
  63.7 2.9 %collective-permute-start.10 = (f32[8,4,8,512]{3,2,1,0:T(8,128)S(1)}, f32[8,4,8,512]{3,2,1,0:T(8,128)S(1)}, u32[]{:S(2)}, u32[]{:S(2)}) collective-permute-start(f32[8,4,8,512]{3,2,1,0:T(8,128)S(1)} %collective-permute-done.7.refs_6_), channel_id=1, source_target_pairs={{0,32},{32,0},{64,96},{96,64},{128,160},{160,128},{192,224},{224,1... | collective-permute-start | bytes 1572872 | tf_op jit(solution)/shard_map/ppermute | solution.py:235

commit v5 on v4

--- a/solution.py
+++ b/solution.py
@@ -216,7 +216,7 @@
                 for k in range(count):
                     fields = [tile[s, k, :, lanes] for lanes in parts]
                     for i in range(count):
-                        factor = factors_ref[i, pl.ds(start + k, deep, stride=0), :]
+                        factor = jnp.broadcast_to(factors_ref[i, pl.ds(start + k, 1), :], (deep, 128))
                         totals[i] = [total + factor * field for total, field in zip(totals[i], fields)]
             for i in range(count):
                 for lanes, total in zip(parts, totals[i]):

time: 69.4 us -> 69.4 us (level)
  no operation moved by 1% of the time
where the time goes in v5:
time: 69.4 us; the launch traced here: 69.2 us
  blocking collectives  41.6 us (60%)
  starting transfers between devices  16.9 us (24%)
  Pallas kernels  8.97 us (13%)
  between operations  1.44 us (2%)
    ppermute x11, starting transfers between devices, swapped(): lax.ppermute(value, axis, [(i, partner(i)) for i in range(lax.axis_size(a...  16.9 us
    all_to_all x1, blocking collectives, body(): gram = jnp.sum(lax.all_to_all(gram, ('lx', 'ly'), 0, 0), axis=0)  16.6 us
    all_to_all x1, blocking collectives, body(): mine = lax.all_to_all(strips, 'grp', 0, 0).reshape(every, deep, cols)  15.5 us
    all_to_all x1, blocking collectives, body(): lax.all_to_all(jnp.broadcast_to(gram[None], (groups,) + gram.shape), 'grp...  9.55 us
    pallas_call x1, Pallas kernels, body(): pl.pallas_call(combine_kernel, out_shape=shape_of(count, rows, cols), in_...  2.51 us
    pallas_call x1, Pallas kernels, body(): pl.pallas_call(lambda *refs: factor_kernel(1.0 / total, *refs), out_shape...  2.42 us
    pallas_call x1, Pallas kernels, body(): pl.pallas_call(filter_kernel, out_shape=(vmem_shape_of(groups, count, dee...  2.04 us
  transfers between devices with their start and end apart: 11, of which 1 were waited for; matrix products, arithmetic and copies ran while one was open for 0% of the time, Pallas kernels for 4%

profile of v5, /device:TPU:1, one launch (start us, length us, event | category | flops | bytes accessed | tf_op | source)
XLA Modules:
  0.0 69.2 jit_solution(7151889596860609045)
XLA Ops:
  0.0 0.1 stack.35.place_ref.refs_1_
  0.1 0.0 copy-start
  0.1 0.0 copy-start.1
  0.1 1.3 %edges.1 = (f32[40,128]{1,0:T(8,128)S(1)}, f32[40,128]{1,0:T(8,128)S(1)}, f32[8,128]{1,0:T(8,128)S(1)}, f32[8,128]{1,0:T(8,128)S(1)}) custom-call(s32[8]{0:T(128)S(1)} %stack.35.place_ref.refs_1_, f32[4,64,512]{2,1,0:T(8,128)} %v_ref.1, f32[4,64,512]{2,1,0:T(8,128)} %v_ref.1, f32[4,64,512]{2,1,0:T(8,128)} %v_ref.1, f32[4,64,512]{2,1,0:T(8,128)} %v_ref.1, ...), custom_call_target="tpu_custom_call" | custom-call | tf_op jit(solution)/shard_map/edges/pallas_call | solution.py:263
  1.4 2.2 %collective-permute-start = (f32[40,128]{1,0:T(8,128)S(1)}, f32[40,128]{1,0:T(8,128)S(1)}, u32[]{:S(2)}, u32[]{:S(2)}) collective-permute-start(f32[40,128]{1,0:T(8,128)S(1)} %get-tuple-element.21), channel_id=1, source_target_pairs={{0,8},{8,0},{16,24},{24,16},{1,9},{9,1},{17,25},{25,17},{2,10},{10... | collective-permute-start | bytes 61448 | tf_op jit(solution)/shard_map/ppermute | solution.py:235
  3.6 1.9 %collective-permute-start.1 = (f32[40,128]{1,0:T(8,128)S(1)}, f32[40,128]{1,0:T(8,128)S(1)}, u32[]{:S(2)}, u32[]{:S(2)}) collective-permute-start(f32[40,128]{1,0:T(8,128)S(1)} %get-tuple-element.22), channel_id=1, source_target_pairs={{0,24},{8,16},{16,8},{24,0},{1,25},{9,17},{17,9},{25,1},{2,26},{10... | collective-permute-start | bytes 61448 | tf_op jit(solution)/shard_map/ppermute | solution.py:235
  5.5 1.6 %collective-permute-start.2 = (f32[8,128]{1,0:T(8,128)S(1)}, f32[8,128]{1,0:T(8,128)S(1)}, u32[]{:S(2)}, u32[]{:S(2)}) collective-permute-start(f32[8,128]{1,0:T(8,128)S(1)} %get-tuple-element.23), channel_id=1, source_target_pairs={{0,1},{1,0},{2,3},{3,2},{4,5},{5,4},{6,7},{7,6},{8,9},{9,8},{10,11... | collective-permute-start | bytes 12296 | tf_op jit(solution)/shard_map/ppermute | solution.py:235
  7.2 4.7 %collective-permute-start.3 = (f32[8,128]{1,0:T(8,128)S(1)}, f32[8,128]{1,0:T(8,128)S(1)}, u32[]{:S(2)}, u32[]{:S(2)}) collective-permute-start(f32[8,128]{1,0:T(8,128)S(1)} %get-tuple-element.24), channel_id=1, source_target_pairs={{0,7},{1,2},{2,1},{3,4},{4,3},{5,6},{6,5},{7,0},{8,15},{9,10},{10,... | collective-permute-start | bytes 12296 | tf_op jit(solution)/shard_map/ppermute | solution.py:235
  12.5 0.0 copy-start.2
  13.2 0.0 collective-permute-done.2.near_ref
  13.2 0.0 collective-permute-done.3.far_ref
  13.2 0.0 collective-permute-done.near_rows_ref
  13.2 0.0 collective-permute-done.1.far_rows_ref
  13.2 0.0 copy-done
  13.2 0.0 copy-done.1
  13.2 0.0 copy-done.2
  13.2 2.0 %filter.1 = (f32[8,4,8,512]{3,2,1,0:T(8,128)S(1)}, f32[8,128]{1,0:T(8,128)S(1)}) custom-call(s32[8]{0:T(128)S(1)} %stack.35.place_ref.refs_1_, f32[4,64,512]{2,1,0:T(8,128)S(1)} %copy-done, s32[64,512]{1,0:T(8,128)S(1)} %copy-done.1, f32[8]{0:T(128)S(1)} %copy-done.2, f32[40,128]{1,0:T(8,128)S(1)} %collective-permute-done.near_rows_ref, ...), custom_call_target="tpu_custom_call" | custom-call | tf_op jit(solution)/shard_map/filter/pallas_call | solution.py:284
  15.3 15.5 %all_to_all.15 = f32[8,4,8,512]{3,2,1,0:T(8,128)S(1)} all-to-all(f32[8,4,8,512]{3,2,1,0:T(8,128)S(1)} %get-tuple-element.32.refs_0_), channel_id=1, replica_groups=mesh['grp'=8,'lx'=4,'ly'=8] {'grp'}, dimensions={0} | all-to-all | bytes 1048576 | tf_op jit(solution)/shard_map/all_to_all | solution.py:292
  30.8 0.9 %collective-permute-start.7 = (f32[8,4,8,512]{3,2,1,0:T(8,128)S(1)}, f32[8,4,8,512]{3,2,1,0:T(8,128)S(1)}, u32[]{:S(2)}, u32[]{:S(2)}) collective-permute-start(f32[8,4,8,512]{3,2,1,0:T(8,128)S(1)} %get-tuple-element.32.refs_0_), channel_id=1, source_target_pairs={{0,192},{32,224},{64,128},{96,160},{128,64},{160,96},{192,0},{224,... | collective-permute-start | bytes 1572872 | tf_op jit(solution)/shard_map/ppermute | solution.py:235
  31.6 1.2 %collective-permute-start.6 = (f32[8,4,8,512]{3,2,1,0:T(8,128)S(1)}, f32[8,4,8,512]{3,2,1,0:T(8,128)S(1)}, u32[]{:S(2)}, u32[]{:S(2)}) collective-permute-start(f32[8,4,8,512]{3,2,1,0:T(8,128)S(1)} %get-tuple-element.32.refs_0_), channel_id=1, source_target_pairs={{0,128},{32,160},{64,192},{96,224},{128,0},{160,32},{192,64},{224,... | collective-permute-start | bytes 1572872 | tf_op jit(solution)/shard_map/ppermute | solution.py:235
  32.8 1.2 %collective-permute-start.5 = (f32[8,4,8,512]{3,2,1,0:T(8,128)S(1)}, f32[8,4,8,512]{3,2,1,0:T(8,128)S(1)}, u32[]{:S(2)}, u32[]{:S(2)}) collective-permute-start(f32[8,4,8,512]{3,2,1,0:T(8,128)S(1)} %get-tuple-element.32.refs_0_), channel_id=1, source_target_pairs={{0,64},{32,96},{64,0},{96,32},{128,192},{160,224},{192,128},{224,1... | collective-permute-start | bytes 1572872 | tf_op jit(solution)/shard_map/ppermute | solution.py:235
  34.0 1.9 %collective-permute-start.4 = (f32[8,4,8,512]{3,2,1,0:T(8,128)S(1)}, f32[8,4,8,512]{3,2,1,0:T(8,128)S(1)}, u32[]{:S(2)}, u32[]{:S(2)}) collective-permute-start(f32[8,4,8,512]{3,2,1,0:T(8,128)S(1)} %get-tuple-element.32.refs_0_), channel_id=1, source_target_pairs={{0,32},{32,0},{64,96},{96,64},{128,160},{160,128},{192,224},{224,1... | collective-permute-start | bytes 1572872 | tf_op jit(solution)/shard_map/ppermute | solution.py:235
  35.9 0.7 gram.1
  36.6 16.6 %all_to_all.16 = f32[32,12,128]{2,1,0:T(8,128)S(1)} all-to-all(f32[32,12,128]{2,1,0:T(8,128)S(1)} %gram.1), channel_id=1, replica_groups=mesh['grp'=8,'lx'=4,'ly'=8] {'lx','ly'}, dimensions={0} | all-to-all | bytes 393216 | tf_op jit(solution)/shard_map/all_to_all | solution.py:306
  53.2 9.5 %all_to_all.17.refs_0_ = f32[8,12,128]{2,1,0:T(8,128)S(1)} all-to-all(f32[8,12,128]{2,1,0:T(8,128)S(1)} %broadcast_in_dim.2), channel_id=1, replica_groups=mesh['grp'=8,'lx'=4,'ly'=8] {'grp'}, dimensions={0} | all-to-all | bytes 98304 | tf_op jit(solution)/shard_map/all_to_all | solution.py:307
  62.7 0.0 collective-permute-done.7.refs_6_
  62.7 0.0 collective-permute-done.6.refs_4_
  62.7 0.0 collective-permute-done.5.refs_2_
  62.8 0.0 collective-permute-done.4.refs_1_
  62.8 0.9 %collective-permute-start.8 = (f32[8,4,8,512]{3,2,1,0:T(8,128)S(1)}, f32[8,4,8,512]{3,2,1,0:T(8,128)S(1)}, u32[]{:S(2)}, u32[]{:S(2)}) collective-permute-start(f32[8,4,8,512]{3,2,1,0:T(8,128)S(1)} %collective-permute-done.5.refs_2_), channel_id=1, source_target_pairs={{0,32},{32,0},{64,96},{96,64},{128,160},{160,128},{192,224},{224,1... | collective-permute-start | bytes 1572872 | tf_op jit(solution)/shard_map/ppermute | solution.py:235
  63.6 0.1 collective-permute-start.9
  63.7 0.4 collective-permute-start.10
  64.1 2.4 %factor.1 = (f32[4,32,128]{2,1,0:T(8,128)S(1)}, f32[16,128]{1,0:T(8,128)S(1)}) custom-call(f32[8,12,128]{2,1,0:T(8,128)S(1)} %all_to_all.17.refs_0_, s32[8]{0:T(128)S(1)} %stack.35.place_ref.refs_1_), custom_call_target="tpu_custom_call" | custom-call | tf_op jit(solution)/shard_map/factor/pallas_call | solution.py:311
  66.6 0.0 collective-permute-done.8.refs_3_
  66.6 0.0 collective-permute-done.9.refs_5_
  66.6 0.1 collective-permute-done.10.refs_7_
  66.7 2.5 %combine.1 = f32[4,64,512]{2,1,0:T(8,128)} custom-call(f32[4,32,128]{2,1,0:T(8,128)S(1)} %get-tuple-element.30.factors_ref, f32[16,128]{1,0:T(8,128)S(1)} %get-tuple-element.31.corners_ref, s32[8]{0:T(128)S(1)} %stack.35.place_ref.refs_1_, f32[8,4,8,512]{3,2,1,0:T(8,128)S(1)} %get-tuple-element.32.refs_0_, ...), custom_call_target="tpu_custom_call" | custom-call | tf_op jit(solution)/shard_map/combine/pallas_call | solution.py:319
  (2 shorter events, 0.0 us)
Async XLA Ops:
  0.1 13.1 %copy-start = (f32[4,64,512]{2,1,0:T(8,128)S(1)}, f32[4,64,512]{2,1,0:T(8,128)}, u32[]{:S(2)}) copy-start(f32[4,64,512]{2,1,0:T(8,128)} %v_ref.1) | copy-start | bytes 1572868
  0.1 13.1 %copy-start.1 = (s32[64,512]{1,0:T(8,128)S(1)}, s32[64,512]{1,0:T(8,128)}, u32[]{:S(2)}) copy-start(s32[64,512]{1,0:T(8,128)} %levels_ref.1) | copy-start | bytes 393220
  1.4 11.8 %collective-permute-start = (f32[40,128]{1,0:T(8,128)S(1)}, f32[40,128]{1,0:T(8,128)S(1)}, u32[]{:S(2)}, u32[]{:S(2)}) collective-permute-start(f32[40,128]{1,0:T(8,128)S(1)} %get-tuple-element.21), channel_id=1, source_target_pairs={{0,8},{8,0},{16,24},{24,16},{1,9},{9,1},{17,25},{25,17},{2,10},{10... | collective-permute-start | bytes 61448 | tf_op jit(solution)/shard_map/ppermute | solution.py:235
  3.6 9.6 %collective-permute-start.1 = (f32[40,128]{1,0:T(8,128)S(1)}, f32[40,128]{1,0:T(8,128)S(1)}, u32[]{:S(2)}, u32[]{:S(2)}) collective-permute-start(f32[40,128]{1,0:T(8,128)S(1)} %get-tuple-element.22), channel_id=1, source_target_pairs={{0,24},{8,16},{16,8},{24,0},{1,25},{9,17},{17,9},{25,1},{2,26},{10... | collective-permute-start | bytes 61448 | tf_op jit(solution)/shard_map/ppermute | solution.py:235
  5.5 7.6 %collective-permute-start.2 = (f32[8,128]{1,0:T(8,128)S(1)}, f32[8,128]{1,0:T(8,128)S(1)}, u32[]{:S(2)}, u32[]{:S(2)}) collective-permute-start(f32[8,128]{1,0:T(8,128)S(1)} %get-tuple-element.23), channel_id=1, source_target_pairs={{0,1},{1,0},{2,3},{3,2},{4,5},{5,4},{6,7},{7,6},{8,9},{9,8},{10,11... | collective-permute-start | bytes 12296 | tf_op jit(solution)/shard_map/ppermute | solution.py:235
  7.2 6.0 %collective-permute-start.3 = (f32[8,128]{1,0:T(8,128)S(1)}, f32[8,128]{1,0:T(8,128)S(1)}, u32[]{:S(2)}, u32[]{:S(2)}) collective-permute-start(f32[8,128]{1,0:T(8,128)S(1)} %get-tuple-element.24), channel_id=1, source_target_pairs={{0,7},{1,2},{2,1},{3,4},{4,3},{5,6},{6,5},{7,0},{8,15},{9,10},{10,... | collective-permute-start | bytes 12296 | tf_op jit(solution)/shard_map/ppermute | solution.py:235
  12.5 0.7 %copy-start.2 = (f32[8]{0:T(128)S(1)}, f32[8]{0:T(128)}, u32[]{:S(2)}) copy-start(f32[8]{0:T(128)} %table_ref.1) | copy-start | bytes 100
  30.8 32.0 %collective-permute-start.7 = (f32[8,4,8,512]{3,2,1,0:T(8,128)S(1)}, f32[8,4,8,512]{3,2,1,0:T(8,128)S(1)}, u32[]{:S(2)}, u32[]{:S(2)}) collective-permute-start(f32[8,4,8,512]{3,2,1,0:T(8,128)S(1)} %get-tuple-element.32.refs_0_), channel_id=1, source_target_pairs={{0,192},{32,224},{64,128},{96,160},{128,64},{160,96},{192,0},{224,... | collective-permute-start | bytes 1572872 | tf_op jit(solution)/shard_map/ppermute | solution.py:235
  31.6 31.1 %collective-permute-start.6 = (f32[8,4,8,512]{3,2,1,0:T(8,128)S(1)}, f32[8,4,8,512]{3,2,1,0:T(8,128)S(1)}, u32[]{:S(2)}, u32[]{:S(2)}) collective-permute-start(f32[8,4,8,512]{3,2,1,0:T(8,128)S(1)} %get-tuple-element.32.refs_0_), channel_id=1, source_target_pairs={{0,128},{32,160},{64,192},{96,224},{128,0},{160,32},{192,64},{224,... | collective-permute-start | bytes 1572872 | tf_op jit(solution)/shard_map/ppermute | solution.py:235
  32.8 29.9 %collective-permute-start.5 = (f32[8,4,8,512]{3,2,1,0:T(8,128)S(1)}, f32[8,4,8,512]{3,2,1,0:T(8,128)S(1)}, u32[]{:S(2)}, u32[]{:S(2)}) collective-permute-start(f32[8,4,8,512]{3,2,1,0:T(8,128)S(1)} %get-tuple-element.32.refs_0_), channel_id=1, source_target_pairs={{0,64},{32,96},{64,0},{96,32},{128,192},{160,224},{192,128},{224,1... | collective-permute-start | bytes 1572872 | tf_op jit(solution)/shard_map/ppermute | solution.py:235
  34.0 28.7 %collective-permute-start.4 = (f32[8,4,8,512]{3,2,1,0:T(8,128)S(1)}, f32[8,4,8,512]{3,2,1,0:T(8,128)S(1)}, u32[]{:S(2)}, u32[]{:S(2)}) collective-permute-start(f32[8,4,8,512]{3,2,1,0:T(8,128)S(1)} %get-tuple-element.32.refs_0_), channel_id=1, source_target_pairs={{0,32},{32,0},{64,96},{96,64},{128,160},{160,128},{192,224},{224,1... | collective-permute-start | bytes 1572872 | tf_op jit(solution)/shard_map/ppermute | solution.py:235
  62.8 3.8 %collective-permute-start.8 = (f32[8,4,8,512]{3,2,1,0:T(8,128)S(1)}, f32[8,4,8,512]{3,2,1,0:T(8,128)S(1)}, u32[]{:S(2)}, u32[]{:S(2)}) collective-permute-start(f32[8,4,8,512]{3,2,1,0:T(8,128)S(1)} %collective-permute-done.5.refs_2_), channel_id=1, source_target_pairs={{0,32},{32,0},{64,96},{96,64},{128,160},{160,128},{192,224},{224,1... | collective-permute-start | bytes 1572872 | tf_op jit(solution)/shard_map/ppermute | solution.py:235
  63.6 3.0 %collective-permute-start.9 = (f32[8,4,8,512]{3,2,1,0:T(8,128)S(1)}, f32[8,4,8,512]{3,2,1,0:T(8,128)S(1)}, u32[]{:S(2)}, u32[]{:S(2)}) collective-permute-start(f32[8,4,8,512]{3,2,1,0:T(8,128)S(1)} %collective-permute-done.6.refs_4_), channel_id=1, source_target_pairs={{0,32},{32,0},{64,96},{96,64},{128,160},{160,128},{192,224},{224,1... | collective-permute-start | bytes 1572872 | tf_op jit(solution)/shard_map/ppermute | solution.py:235
  63.7 2.9 %collective-permute-start.10 = (f32[8,4,8,512]{3,2,1,0:T(8,128)S(1)}, f32[8,4,8,512]{3,2,1,0:T(8,128)S(1)}, u32[]{:S(2)}, u32[]{:S(2)}) collective-permute-start(f32[8,4,8,512]{3,2,1,0:T(8,128)S(1)} %collective-permute-done.7.refs_6_), channel_id=1, source_target_pairs={{0,32},{32,0},{64,96},{96,64},{128,160},{160,128},{192,224},{224,1... | collective-permute-start | bytes 1572872 | tf_op jit(solution)/shard_map/ppermute | solution.py:235

commit v6 on v5

--- a/solution.py
+++ b/solution.py
@@ -291,7 +291,7 @@
     )(place, vectors, levels, level_table, near_rows, far_rows, near, far, filter_low, filter_high)
     mine = lax.all_to_all(strips, "grp", 0, 0).reshape(every, deep, cols)
     strips, mine = lax.optimization_barrier((strips, mine))
-    tiles = {q: swapped(strips, "grp", lambda i, q=q: i ^ q) for q in (1, 4, 2, 6)}
+    tiles = {q: swapped(strips, "grp", lambda i, q=q: i ^ q) for q in (4, 2, 6)}
     tiles[0] = strips
     planes = lax.axis_size("lx") * lax.axis_size("ly")
     total = rows * cols * planes
@@ -306,7 +306,7 @@
     gram = jnp.sum(lax.all_to_all(gram, ("lx", "ly"), 0, 0), axis=0)
     grams = lax.all_to_all(jnp.broadcast_to(gram[None], (groups,) + gram.shape), "grp", 0, 0)
     grams, tiles = lax.optimization_barrier((grams, tiles))
-    for q in range(2, groups, 2):
+    for q in range(0, groups, 2):
         tiles[q + 1] = swapped(tiles[q], "grp", lambda i: i ^ 1)
     factors, corners = pl.pallas_call(
         lambda *refs: factor_kernel(1.0 / total, *refs),

time: 69.4 us -> 69 us (level)
  starting transfers between devices: 16.9 us -> 15.1 us
  blocking collectives: 41.6 us -> 42.4 us
    ppermute x11, starting transfers between devices: 16.9 us -> 15.1 us  [swapped(): lax.ppermute(value, axis, [(i, partner(i)) for i in range(lax.axis_size(a...]
    all_to_all x1, blocking collectives: 9.55 us -> 11 us  [body(): lax.all_to_all(jnp.broadcast_to(gram[None], (groups,) + gram.shape), 'grp...]
where the time goes in v6:
time: 69 us; the launch traced here: 68.8 us
  blocking collectives  42.4 us (61%)
  starting transfers between devices  15.1 us (22%)
  Pallas kernels  8.97 us (13%)
  between operations  1.44 us (2%)
  waiting for transfers between devices  0.74 us (1%)
    all_to_all x1, blocking collectives, body(): gram = jnp.sum(lax.all_to_all(gram, ('lx', 'ly'), 0, 0), axis=0)  15.9 us
    all_to_all x1, blocking collectives, body(): mine = lax.all_to_all(strips, 'grp', 0, 0).reshape(every, deep, cols)  15.5 us
    ppermute x11, starting transfers between devices, swapped(): lax.ppermute(value, axis, [(i, partner(i)) for i in range(lax.axis_size(a...  15.1 us
    all_to_all x1, blocking collectives, body(): lax.all_to_all(jnp.broadcast_to(gram[None], (groups,) + gram.shape), 'grp...  11 us
    pallas_call x1, Pallas kernels, body(): pl.pallas_call(combine_kernel, out_shape=shape_of(count, rows, cols), in_...  2.51 us
    pallas_call x1, Pallas kernels, body(): pl.pallas_call(lambda *refs: factor_kernel(1.0 / total, *refs), out_shape...  2.42 us
    pallas_call x1, Pallas kernels, body(): pl.pallas_call(filter_kernel, out_shape=(vmem_shape_of(groups, count, dee...  2.04 us
  transfers between devices with their start and end apart: 11, of which 1 were waited for; matrix products, arithmetic and copies ran while one was open for 0% of the time, Pallas kernels for 4%

profile of v6, /device:TPU:1, one launch (start us, length us, event | category | flops | bytes accessed | tf_op | source)
XLA Modules:
  0.0 68.8 jit_solution(16919501463685712822)
XLA Ops:
  0.0 0.1 stack.35.place_ref.refs_1_
  0.1 0.0 copy-start
  0.1 0.0 copy-start.1
  0.1 1.3 %edges.1 = (f32[40,128]{1,0:T(8,128)S(1)}, f32[40,128]{1,0:T(8,128)S(1)}, f32[8,128]{1,0:T(8,128)S(1)}, f32[8,128]{1,0:T(8,128)S(1)}) custom-call(s32[8]{0:T(128)S(1)} %stack.35.place_ref.refs_1_, f32[4,64,512]{2,1,0:T(8,128)} %v_ref.1, f32[4,64,512]{2,1,0:T(8,128)} %v_ref.1, f32[4,64,512]{2,1,0:T(8,128)} %v_ref.1, f32[4,64,512]{2,1,0:T(8,128)} %v_ref.1, ...), custom_call_target="tpu_custom_call" | custom-call | tf_op jit(solution)/shard_map/edges/pallas_call | solution.py:263
  1.4 2.2 %collective-permute-start = (f32[40,128]{1,0:T(8,128)S(1)}, f32[40,128]{1,0:T(8,128)S(1)}, u32[]{:S(2)}, u32[]{:S(2)}) collective-permute-start(f32[40,128]{1,0:T(8,128)S(1)} %get-tuple-element.20), channel_id=1, source_target_pairs={{0,8},{8,0},{16,24},{24,16},{1,9},{9,1},{17,25},{25,17},{2,10},{10... | collective-permute-start | bytes 61448 | tf_op jit(solution)/shard_map/ppermute | solution.py:235
  3.6 1.9 %collective-permute-start.1 = (f32[40,128]{1,0:T(8,128)S(1)}, f32[40,128]{1,0:T(8,128)S(1)}, u32[]{:S(2)}, u32[]{:S(2)}) collective-permute-start(f32[40,128]{1,0:T(8,128)S(1)} %get-tuple-element.21), channel_id=1, source_target_pairs={{0,24},{8,16},{16,8},{24,0},{1,25},{9,17},{17,9},{25,1},{2,26},{10... | collective-permute-start | bytes 61448 | tf_op jit(solution)/shard_map/ppermute | solution.py:235
  5.5 1.6 %collective-permute-start.2 = (f32[8,128]{1,0:T(8,128)S(1)}, f32[8,128]{1,0:T(8,128)S(1)}, u32[]{:S(2)}, u32[]{:S(2)}) collective-permute-start(f32[8,128]{1,0:T(8,128)S(1)} %get-tuple-element.22), channel_id=1, source_target_pairs={{0,1},{1,0},{2,3},{3,2},{4,5},{5,4},{6,7},{7,6},{8,9},{9,8},{10,11... | collective-permute-start | bytes 12296 | tf_op jit(solution)/shard_map/ppermute | solution.py:235
  7.2 4.7 %collective-permute-start.3 = (f32[8,128]{1,0:T(8,128)S(1)}, f32[8,128]{1,0:T(8,128)S(1)}, u32[]{:S(2)}, u32[]{:S(2)}) collective-permute-start(f32[8,128]{1,0:T(8,128)S(1)} %get-tuple-element.23), channel_id=1, source_target_pairs={{0,7},{1,2},{2,1},{3,4},{4,3},{5,6},{6,5},{7,0},{8,15},{9,10},{10,... | collective-permute-start | bytes 12296 | tf_op jit(solution)/shard_map/ppermute | solution.py:235
  12.5 0.0 copy-start.2
  13.2 0.0 collective-permute-done.2.near_ref
  13.2 0.0 collective-permute-done.3.far_ref
  13.2 0.0 collective-permute-done.near_rows_ref
  13.2 0.0 collective-permute-done.1.far_rows_ref
  13.2 0.0 copy-done
  13.2 0.0 copy-done.1
  13.2 0.0 copy-done.2
  13.2 2.0 %filter.1 = (f32[8,4,8,512]{3,2,1,0:T(8,128)S(1)}, f32[8,128]{1,0:T(8,128)S(1)}) custom-call(s32[8]{0:T(128)S(1)} %stack.35.place_ref.refs_1_, f32[4,64,512]{2,1,0:T(8,128)S(1)} %copy-done, s32[64,512]{1,0:T(8,128)S(1)} %copy-done.1, f32[8]{0:T(128)S(1)} %copy-done.2, f32[40,128]{1,0:T(8,128)S(1)} %collective-permute-done.near_rows_ref, ...), custom_call_target="tpu_custom_call" | custom-call | tf_op jit(solution)/shard_map/filter/pallas_call | solution.py:284
  15.3 15.5 %all_to_all.15 = f32[8,4,8,512]{3,2,1,0:T(8,128)S(1)} all-to-all(f32[8,4,8,512]{3,2,1,0:T(8,128)S(1)} %get-tuple-element.31.refs_0_), channel_id=1, replica_groups=mesh['grp'=8,'lx'=4,'ly'=8] {'grp'}, dimensions={0} | all-to-all | bytes 1048576 | tf_op jit(solution)/shard_map/all_to_all | solution.py:292
  30.8 0.9 %collective-permute-start.6 = (f32[8,4,8,512]{3,2,1,0:T(8,128)S(1)}, f32[8,4,8,512]{3,2,1,0:T(8,128)S(1)}, u32[]{:S(2)}, u32[]{:S(2)}) collective-permute-start(f32[8,4,8,512]{3,2,1,0:T(8,128)S(1)} %get-tuple-element.31.refs_0_), channel_id=1, source_target_pairs={{0,192},{32,224},{64,128},{96,160},{128,64},{160,96},{192,0},{224,... | collective-permute-start | bytes 1572872 | tf_op jit(solution)/shard_map/ppermute | solution.py:235
  31.6 1.2 %collective-permute-start.5 = (f32[8,4,8,512]{3,2,1,0:T(8,128)S(1)}, f32[8,4,8,512]{3,2,1,0:T(8,128)S(1)}, u32[]{:S(2)}, u32[]{:S(2)}) collective-permute-start(f32[8,4,8,512]{3,2,1,0:T(8,128)S(1)} %get-tuple-element.31.refs_0_), channel_id=1, source_target_pairs={{0,128},{32,160},{64,192},{96,224},{128,0},{160,32},{192,64},{224,... | collective-permute-start | bytes 1572872 | tf_op jit(solution)/shard_map/ppermute | solution.py:235
  32.8 1.2 %collective-permute-start.4 = (f32[8,4,8,512]{3,2,1,0:T(8,128)S(1)}, f32[8,4,8,512]{3,2,1,0:T(8,128)S(1)}, u32[]{:S(2)}, u32[]{:S(2)}) collective-permute-start(f32[8,4,8,512]{3,2,1,0:T(8,128)S(1)} %get-tuple-element.31.refs_0_), channel_id=1, source_target_pairs={{0,64},{32,96},{64,0},{96,32},{128,192},{160,224},{192,128},{224,1... | collective-permute-start | bytes 1572872 | tf_op jit(solution)/shard_map/ppermute | solution.py:235
  34.0 0.7 gram.1
  34.7 15.9 %all_to_all.16 = f32[32,12,128]{2,1,0:T(8,128)S(1)} all-to-all(f32[32,12,128]{2,1,0:T(8,128)S(1)} %gram.1), channel_id=1, replica_groups=mesh['grp'=8,'lx'=4,'ly'=8] {'lx','ly'}, dimensions={0} | all-to-all | bytes 393216 | tf_op jit(solution)/shard_map/all_to_all | solution.py:306
  50.7 11.0 %all_to_all.17.refs_0_ = f32[8,12,128]{2,1,0:T(8,128)S(1)} all-to-all(f32[8,12,128]{2,1,0:T(8,128)S(1)} %broadcast_in_dim.2), channel_id=1, replica_groups=mesh['grp'=8,'lx'=4,'ly'=8] {'grp'}, dimensions={0} | all-to-all | bytes 98304 | tf_op jit(solution)/shard_map/all_to_all | solution.py:307
  61.6 0.0 collective-permute-done.6.refs_6_
  61.6 0.0 collective-permute-done.5.refs_4_
  61.6 0.0 collective-permute-done.4.refs_2_
  61.6 0.9 %collective-permute-start.7 = (f32[8,4,8,512]{3,2,1,0:T(8,128)S(1)}, f32[8,4,8,512]{3,2,1,0:T(8,128)S(1)}, u32[]{:S(2)}, u32[]{:S(2)}) collective-permute-start(f32[8,4,8,512]{3,2,1,0:T(8,128)S(1)} %get-tuple-element.31.refs_0_), channel_id=1, source_target_pairs={{0,32},{32,0},{64,96},{96,64},{128,160},{160,128},{192,224},{224,1... | collective-permute-start | bytes 1572872 | tf_op jit(solution)/shard_map/ppermute | solution.py:235
  62.5 0.1 collective-permute-start.8
  62.6 0.4 collective-permute-start.9
  63.0 0.1 collective-permute-start.10
  63.1 2.4 %factor.1 = (f32[4,32,128]{2,1,0:T(8,128)S(1)}, f32[16,128]{1,0:T(8,128)S(1)}) custom-call(f32[8,12,128]{2,1,0:T(8,128)S(1)} %all_to_all.17.refs_0_, s32[8]{0:T(128)S(1)} %stack.35.place_ref.refs_1_), custom_call_target="tpu_custom_call" | custom-call | tf_op jit(solution)/shard_map/factor/pallas_call | solution.py:311
  65.5 0.0 collective-permute-done.7.refs_1_
  65.6 0.0 collective-permute-done.8.refs_3_
  65.6 0.0 collective-permute-done.9.refs_5_
  65.6 0.7 %collective-permute-done.10.refs_7_ = f32[8,4,8,512]{3,2,1,0:T(8,128)S(1)} collective-permute-done((f32[8,4,8,512]{3,2,1,0:T(8,128)S(1)}, f32[8,4,8,512]{3,2,1,0:T(8,128)S(1)}, u32[]{:S(2)}, u32[]{:S(2)}) %collective-permute-start.10) | collective-permute-done | bytes 524320 | tf_op jit(solution)/shard_map/ppermute | solution.py:235
  66.3 2.5 %combine.1 = f32[4,64,512]{2,1,0:T(8,128)} custom-call(f32[4,32,128]{2,1,0:T(8,128)S(1)} %get-tuple-element.29.factors_ref, f32[16,128]{1,0:T(8,128)S(1)} %get-tuple-element.30.corners_ref, s32[8]{0:T(128)S(1)} %stack.35.place_ref.refs_1_, f32[8,4,8,512]{3,2,1,0:T(8,128)S(1)} %get-tuple-element.31.refs_0_, ...), custom_call_target="tpu_custom_call" | custom-call | tf_op jit(solution)/shard_map/combine/pallas_call | solution.py:319
  (2 shorter events, 0.0 us)
Async XLA Ops:
  0.1 13.1 %copy-start = (f32[4,64,512]{2,1,0:T(8,128)S(1)}, f32[4,64,512]{2,1,0:T(8,128)}, u32[]{:S(2)}) copy-start(f32[4,64,512]{2,1,0:T(8,128)} %v_ref.1) | copy-start | bytes 1572868
  0.1 13.1 %copy-start.1 = (s32[64,512]{1,0:T(8,128)S(1)}, s32[64,512]{1,0:T(8,128)}, u32[]{:S(2)}) copy-start(s32[64,512]{1,0:T(8,128)} %levels_ref.1) | copy-start | bytes 393220
  1.4 11.8 %collective-permute-start = (f32[40,128]{1,0:T(8,128)S(1)}, f32[40,128]{1,0:T(8,128)S(1)}, u32[]{:S(2)}, u32[]{:S(2)}) collective-permute-start(f32[40,128]{1,0:T(8,128)S(1)} %get-tuple-element.20), channel_id=1, source_target_pairs={{0,8},{8,0},{16,24},{24,16},{1,9},{9,1},{17,25},{25,17},{2,10},{10... | collective-permute-start | bytes 61448 | tf_op jit(solution)/shard_map/ppermute | solution.py:235
  3.6 9.6 %collective-permute-start.1 = (f32[40,128]{1,0:T(8,128)S(1)}, f32[40,128]{1,0:T(8,128)S(1)}, u32[]{:S(2)}, u32[]{:S(2)}) collective-permute-start(f32[40,128]{1,0:T(8,128)S(1)} %get-tuple-element.21), channel_id=1, source_target_pairs={{0,24},{8,16},{16,8},{24,0},{1,25},{9,17},{17,9},{25,1},{2,26},{10... | collective-permute-start | bytes 61448 | tf_op jit(solution)/shard_map/ppermute | solution.py:235
  5.5 7.6 %collective-permute-start.2 = (f32[8,128]{1,0:T(8,128)S(1)}, f32[8,128]{1,0:T(8,128)S(1)}, u32[]{:S(2)}, u32[]{:S(2)}) collective-permute-start(f32[8,128]{1,0:T(8,128)S(1)} %get-tuple-element.22), channel_id=1, source_target_pairs={{0,1},{1,0},{2,3},{3,2},{4,5},{5,4},{6,7},{7,6},{8,9},{9,8},{10,11... | collective-permute-start | bytes 12296 | tf_op jit(solution)/shard_map/ppermute | solution.py:235
  7.2 6.0 %collective-permute-start.3 = (f32[8,128]{1,0:T(8,128)S(1)}, f32[8,128]{1,0:T(8,128)S(1)}, u32[]{:S(2)}, u32[]{:S(2)}) collective-permute-start(f32[8,128]{1,0:T(8,128)S(1)} %get-tuple-element.23), channel_id=1, source_target_pairs={{0,7},{1,2},{2,1},{3,4},{4,3},{5,6},{6,5},{7,0},{8,15},{9,10},{10,... | collective-permute-start | bytes 12296 | tf_op jit(solution)/shard_map/ppermute | solution.py:235
  12.5 0.7 %copy-start.2 = (f32[8]{0:T(128)S(1)}, f32[8]{0:T(128)}, u32[]{:S(2)}) copy-start(f32[8]{0:T(128)} %table_ref.1) | copy-start | bytes 100
  30.8 30.9 %collective-permute-start.6 = (f32[8,4,8,512]{3,2,1,0:T(8,128)S(1)}, f32[8,4,8,512]{3,2,1,0:T(8,128)S(1)}, u32[]{:S(2)}, u32[]{:S(2)}) collective-permute-start(f32[8,4,8,512]{3,2,1,0:T(8,128)S(1)} %get-tuple-element.31.refs_0_), channel_id=1, source_target_pairs={{0,192},{32,224},{64,128},{96,160},{128,64},{160,96},{192,0},{224,... | collective-permute-start | bytes 1572872 | tf_op jit(solution)/shard_map/ppermute | solution.py:235
  31.6 30.0 %collective-permute-start.5 = (f32[8,4,8,512]{3,2,1,0:T(8,128)S(1)}, f32[8,4,8,512]{3,2,1,0:T(8,128)S(1)}, u32[]{:S(2)}, u32[]{:S(2)}) collective-permute-start(f32[8,4,8,512]{3,2,1,0:T(8,128)S(1)} %get-tuple-element.31.refs_0_), channel_id=1, source_target_pairs={{0,128},{32,160},{64,192},{96,224},{128,0},{160,32},{192,64},{224,... | collective-permute-start | bytes 1572872 | tf_op jit(solution)/shard_map/ppermute | solution.py:235
  32.8 28.8 %collective-permute-start.4 = (f32[8,4,8,512]{3,2,1,0:T(8,128)S(1)}, f32[8,4,8,512]{3,2,1,0:T(8,128)S(1)}, u32[]{:S(2)}, u32[]{:S(2)}) collective-permute-start(f32[8,4,8,512]{3,2,1,0:T(8,128)S(1)} %get-tuple-element.31.refs_0_), channel_id=1, source_target_pairs={{0,64},{32,96},{64,0},{96,32},{128,192},{160,224},{192,128},{224,1... | collective-permute-start | bytes 1572872 | tf_op jit(solution)/shard_map/ppermute | solution.py:235
  61.6 3.9 %collective-permute-start.7 = (f32[8,4,8,512]{3,2,1,0:T(8,128)S(1)}, f32[8,4,8,512]{3,2,1,0:T(8,128)S(1)}, u32[]{:S(2)}, u32[]{:S(2)}) collective-permute-start(f32[8,4,8,512]{3,2,1,0:T(8,128)S(1)} %get-tuple-element.31.refs_0_), channel_id=1, source_target_pairs={{0,32},{32,0},{64,96},{96,64},{128,160},{160,128},{192,224},{224,1... | collective-permute-start | bytes 1572872 | tf_op jit(solution)/shard_map/ppermute | solution.py:235
  62.5 3.1 %collective-permute-start.8 = (f32[8,4,8,512]{3,2,1,0:T(8,128)S(1)}, f32[8,4,8,512]{3,2,1,0:T(8,128)S(1)}, u32[]{:S(2)}, u32[]{:S(2)}) collective-permute-start(f32[8,4,8,512]{3,2,1,0:T(8,128)S(1)} %collective-permute-done.4.refs_2_), channel_id=1, source_target_pairs={{0,32},{32,0},{64,96},{96,64},{128,160},{160,128},{192,224},{224,1... | collective-permute-start | bytes 1572872 | tf_op jit(solution)/shard_map/ppermute | solution.py:235
  62.6 3.0 %collective-permute-start.9 = (f32[8,4,8,512]{3,2,1,0:T(8,128)S(1)}, f32[8,4,8,512]{3,2,1,0:T(8,128)S(1)}, u32[]{:S(2)}, u32[]{:S(2)}) collective-permute-start(f32[8,4,8,512]{3,2,1,0:T(8,128)S(1)} %collective-permute-done.5.refs_4_), channel_id=1, source_target_pairs={{0,32},{32,0},{64,96},{96,64},{128,160},{160,128},{192,224},{224,1... | collective-permute-start | bytes 1572872 | tf_op jit(solution)/shard_map/ppermute | solution.py:235
  63.0 3.3 %collective-permute-start.10 = (f32[8,4,8,512]{3,2,1,0:T(8,128)S(1)}, f32[8,4,8,512]{3,2,1,0:T(8,128)S(1)}, u32[]{:S(2)}, u32[]{:S(2)}) collective-permute-start(f32[8,4,8,512]{3,2,1,0:T(8,128)S(1)} %collective-permute-done.6.refs_6_), channel_id=1, source_target_pairs={{0,32},{32,0},{64,96},{96,64},{128,160},{160,128},{192,224},{224,1... | collective-permute-start | bytes 1572872 | tf_op jit(solution)/shard_map/ppermute | solution.py:235
